TPU v7x, 1024 devices: a whole 4x4x32 slice. The times are simulated.
1024 devices in a mesh: dp: 4 (over x_lo, core), context: 32 (over z), tensor: 8 (over x_hi, y).
Axes of the slice: x: 4 (x_hi: 2, x_lo: 2; x = x_hi * 2 + x_lo), y: 4, z: 32, core: 2. Of those that a mesh axis runs over, the one named last changes fastest.
Arguments:
- normed: bfloat16 [4, 12288, 8192], P('dp', 'context', 'tensor'), may hold values from -8 to 8
- frozen_query_base: bfloat16 [4, 12288, 8192], P('dp', 'context', 'tensor'), may hold values from -66 to 66
- frozen_key_base: bfloat16 [4, 12288, 1024], P('dp', 'context', 'tensor'), may hold values from -3 to 3
- frozen_value_base: bfloat16 [4, 12288, 1024], P('dp', 'context', 'tensor'), may hold values from -4 to 4
- adapter_down_weight: bfloat16 [8192, 48], P('tensor'), may hold values from -0.0625 to 0.0625
- query_up_weight: bfloat16 [16, 8192], P(None, 'tensor'), may hold values from -0.29882812 to 0.29882812
- key_value_up_weight: bfloat16 [2, 16, 1024], P(None, None, 'tensor'), may hold values from -0.29882812 to 0.29882812
- output_gradient: bfloat16 [4, 12288, 8192], P('dp', 'context', 'tensor'), may hold values from -0.02734375 to 0.02734375
Outputs:
- attended: bfloat16 [4, 12288, 8192], P('dp', 'context', 'tensor')
- grad_a: float32 [8192, 48], P('tensor')
- query_up_gradient: float32 [16, 8192], P(None, 'tensor')
- grad_bkv: float32 [2, 16, 1024], P(None, None, 'tensor')
All inputs are finite; a program needn't handle non-finite values.
Results may differ from a plain program's by a relative error of at most 0.012.
Values may be sent and summed in bfloat16 or wider, within the bound.
A program may use at most 32 MiB of HBM per device.

v0:
```python
import functools

import jax
import jax.numpy as jnp
from jax import lax
from jax.sharding import Mesh
from jax.sharding import PartitionSpec as P

QUERY_HEAD_COUNT = 64
KEY_VALUE_HEADS = 8
HEAD_SIZE = 128
TENSOR = ("tensor_0", "tensor_1")
DP_CONTEXT = ("dp_0", "dp_1", "context")
DP = ("dp_0", "dp_1")


adapter_scale = 2.0


def cut_along(shard, dim, count):
    dims = shard.shape
    tiles = shard.reshape(*dims[:dim], count, dims[dim] // count, *dims[dim + 1 :])
    return jnp.moveaxis(tiles, dim, 0)


def sent_and_summed(shard, axis, dim):
    count = lax.axis_size(axis)
    tiles = lax.all_to_all(cut_along(shard, dim, count), axis, 0, 0, tiled=True)
    return jnp.sum(tiles, axis=0)


def joined_along(tiles, dim):
    tiles = jnp.moveaxis(tiles, 0, dim)
    dims = tiles.shape
    return tiles.reshape(*dims[:dim], dims[dim] * dims[dim + 1], *dims[dim + 2 :])


def gather_in_order(shard, axes, order):
    tiles = shard
    for k in order:
        tiles = lax.all_gather(tiles, axes[k])
    done = order[::-1]
    back = [done.index(k) for k in range(len(axes))]
    tiles = tiles.transpose(*back, *range(len(axes), tiles.ndim))
    return tiles.reshape(-1, *shard.shape)


def gathered_by_axis(shard, axes, order, dim):
    return joined_along(gather_in_order(shard, axes, order), dim)


def shifted(value, axis, steps):
    count = lax.axis_size(axis)
    pairs = [(source, (source + steps) % count) for source in range(count)]
    return lax.ppermute(value, axis, pairs)


def by_axis(shard, axes):
    return functools.reduce(lax.psum, axes, shard)


def attend_single(query_rows, key_heads, value_heads, grads, allowed):
    scale = HEAD_SIZE ** (-0.5)
    scores = (
        jnp.einsum("tgd,ugd->gtu", query_rows, key_heads, preferred_element_type=jnp.float32)
        * scale
    )
    masked = jnp.where(allowed, scores, -jnp.inf)
    highest = jnp.max(masked, axis=-1, keepdims=True)
    weights = jnp.exp(masked - highest)
    probs = weights / jnp.sum(weights, axis=-1, keepdims=True)
    probs_low = probs.astype(jnp.bfloat16)
    output = jnp.einsum("gtu,ugd->tgd", probs_low, value_heads, preferred_element_type=jnp.float32)
    prob_grad = jnp.einsum("tgd,ugd->gtu", grads, value_heads, preferred_element_type=jnp.float32)
    row_dot = jnp.sum(probs * prob_grad, axis=-1, keepdims=True)
    score_grad = (probs * (prob_grad - row_dot) * scale).astype(jnp.bfloat16)
    query_gradient = jnp.einsum(
        "gtu,ugd->tgd", score_grad, key_heads, preferred_element_type=jnp.float32
    )
    key_gradient = jnp.einsum(
        "gtu,tgd->ugd", score_grad, query_rows, preferred_element_type=jnp.float32
    )
    value_gradient = jnp.einsum(
        "gtu,tgd->ugd", probs_low, grads, preferred_element_type=jnp.float32
    )
    return (output, query_gradient, key_gradient, value_gradient)


def attend(query_rows, key_heads, value_heads, grads, allowed):

    def one_head(pieces):
        return attend_single(pieces[0], key_heads, value_heads, pieces[1], allowed)

    results = lax.map(one_head, (jnp.moveaxis(query_rows, 2, 0), jnp.moveaxis(grads, 2, 0)))
    output = jnp.moveaxis(results[0], 0, 2)
    query_gradient = jnp.moveaxis(results[1], 0, 2)
    key_gradient = jnp.sum(results[2], axis=0)
    value_gradient = jnp.sum(results[3], axis=0)
    return (output, query_gradient, key_gradient, value_gradient)


def head_count_total(partial_sum):
    share = sent_and_summed(partial_sum, TENSOR, 0)
    return gathered_by_axis(share.astype(jnp.bfloat16), TENSOR, (0, 1), 0)


def on_device(
    normed,
    frozen_query_base,
    frozen_key_base,
    frozen_value_base,
    adapter_down_weight,
    query_up_weight,
    key_value_up_weight,
    output_gradient,
):
    token_count = normed[0]
    tok_count = token_count.shape[0]
    half_rows = tok_count // 2
    adapter_depth = query_up_weight.shape[0]
    per_group = QUERY_HEAD_COUNT // KEY_VALUE_HEADS
    half_heads = per_group // 2
    kv_count = frozen_key_base.shape[2] // HEAD_SIZE
    reduced_projection = head_count_total(
        jnp.dot(token_count, adapter_down_weight, preferred_element_type=jnp.float32)
    )
    query_rows = (
        frozen_query_base[0].astype(jnp.float32)
        + adapter_scale
        * jnp.dot(
            reduced_projection[:, :adapter_depth],
            query_up_weight,
            preferred_element_type=jnp.float32,
        )
    ).astype(jnp.bfloat16)
    key_row_block = (
        frozen_key_base[0].astype(jnp.float32)
        + adapter_scale
        * jnp.dot(
            reduced_projection[:, adapter_depth : 2 * adapter_depth],
            key_value_up_weight[0],
            preferred_element_type=jnp.float32,
        )
    ).astype(jnp.bfloat16)
    value_row_block = (
        frozen_value_base[0].astype(jnp.float32)
        + adapter_scale
        * jnp.dot(
            reduced_projection[:, 2 * adapter_depth :],
            key_value_up_weight[1],
            preferred_element_type=jnp.float32,
        )
    ).astype(jnp.bfloat16)
    query_heads = query_rows.reshape(tok_count, kv_count, per_group, HEAD_SIZE)
    grad_heads = output_gradient[0].reshape(tok_count, kv_count, per_group, HEAD_SIZE)
    key_heads = key_row_block.reshape(tok_count, kv_count, HEAD_SIZE)
    value_heads = value_row_block.reshape(tok_count, kv_count, HEAD_SIZE)
    row_ids = lax.broadcasted_iota(jnp.int32, (tok_count, tok_count), 0)
    col_ids = lax.broadcasted_iota(jnp.int32, (tok_count, tok_count), 1)
    causal = col_ids <= row_ids
    straight = attend(
        query_heads[:, :, :half_heads],
        key_heads,
        value_heads,
        grad_heads[:, :, :half_heads],
        causal,
    )
    moved_queries = query_heads[:, :, half_heads:]
    moved_grads = grad_heads[:, :, half_heads:]
    earlier = shifted((key_heads[half_rows:], value_heads[half_rows:]), "context", 1)
    wide_keys = jnp.concatenate([earlier[0], key_heads], axis=0)
    wide_values = jnp.concatenate([earlier[1], value_heads], axis=0)
    wide_rows = lax.broadcasted_iota(jnp.int32, (tok_count, tok_count + half_rows), 0)
    wide_cols = lax.broadcasted_iota(jnp.int32, (tok_count, tok_count + half_rows), 1)
    lower_edge = jnp.where(wide_rows < half_rows, 0, tok_count)
    allowed = (wide_cols >= lower_edge) & (wide_cols <= wide_rows + half_rows)
    wide_parts = attend(moved_queries, wide_keys, wide_values, moved_grads, allowed)
    sent_back = shifted((wide_parts[2][:half_rows], wide_parts[3][:half_rows]), "context", -1)
    zero_rows = jnp.zeros_like(sent_back[0])
    moved_out = wide_parts[0]
    moved_dq = wide_parts[1]
    moved_dk = wide_parts[2][half_rows:] + jnp.concatenate([zero_rows, sent_back[0]], axis=0)
    moved_dv = wide_parts[3][half_rows:] + jnp.concatenate([zero_rows, sent_back[1]], axis=0)
    attended = (
        jnp.concatenate([straight[0], moved_out], axis=2)
        .reshape(tok_count, -1)
        .astype(jnp.bfloat16)
    )
    query_gradient = (
        jnp.concatenate([straight[1], moved_dq], axis=2).reshape(tok_count, -1).astype(jnp.bfloat16)
    )
    key_gradient = (straight[2] + moved_dk).reshape(tok_count, -1).astype(jnp.bfloat16)
    value_gradient = (straight[3] + moved_dv).reshape(tok_count, -1).astype(jnp.bfloat16)
    spanning_axis = (((0,), (0,)), ((), ()))
    query_adapter_gradient = adapter_scale * lax.dot_general(
        reduced_projection[:, :adapter_depth],
        query_gradient,
        spanning_axis,
        preferred_element_type=jnp.float32,
    )
    key_adapter_gradient = adapter_scale * lax.dot_general(
        reduced_projection[:, adapter_depth : 2 * adapter_depth],
        key_gradient,
        spanning_axis,
        preferred_element_type=jnp.float32,
    )
    value_adapter_gradient = adapter_scale * lax.dot_general(
        reduced_projection[:, 2 * adapter_depth :],
        value_gradient,
        spanning_axis,
        preferred_element_type=jnp.float32,
    )
    inner_product = (((1,), (1,)), ((), ()))
    adapter_depth_terms = adapter_scale * jnp.concatenate(
        [
            lax.dot_general(
                query_gradient, query_up_weight, inner_product, preferred_element_type=jnp.float32
            ),
            lax.dot_general(
                key_gradient,
                key_value_up_weight[0],
                inner_product,
                preferred_element_type=jnp.float32,
            ),
            lax.dot_general(
                value_gradient,
                key_value_up_weight[1],
                inner_product,
                preferred_element_type=jnp.float32,
            ),
        ],
        axis=1,
    )
    reduced_projection_gradient = head_count_total(adapter_depth_terms)
    grad_down = lax.dot_general(
        token_count, reduced_projection_gradient, spanning_axis, preferred_element_type=jnp.float32
    )
    grad_a, query_up_gradient, grad_bkv = (
        by_axis(grad_down, DP_CONTEXT),
        by_axis(query_adapter_gradient, DP_CONTEXT),
        by_axis(jnp.stack([key_adapter_gradient, value_adapter_gradient]), DP_CONTEXT),
    )
    return (attended[None], grad_a, query_up_gradient, grad_bkv)


def solution(mesh):
    split = Mesh(
        mesh.devices.reshape(2, 2, mesh.shape["context"], 2, 4),
        ("dp_0", "dp_1", "context", "tensor_0", "tensor_1"),
    )
    placed = (
        P(DP, "context", TENSOR),
        P(DP, "context", TENSOR),
        P(DP, "context", TENSOR),
        P(DP, "context", TENSOR),
        P(TENSOR, None),
        P(None, TENSOR),
        P(None, None, TENSOR),
        P(DP, "context", TENSOR),
    )
    return jax.shard_map(
        on_device,
        mesh=split,
        in_specs=placed,
        out_specs=(
            P(DP, "context", TENSOR),
            P(TENSOR, None),
            P(None, TENSOR),
            P(None, None, TENSOR),
        ),
        check_vma=False,
    )
```

profile of v0, /device:TPU:2, one launch (start us, length us, event | category | flops | bytes accessed | tf_op | source)
XLA Modules:
  0.0 549.0 jit_solution(6504494414153124982)
XLA Ops:
  7.2 1.1 copy-done
  8.3 1.2 fusion.76
  9.5 0.8 reshape.225
  10.4 6.0 %all-to-all-start = ((f32[8,1,2304]{2,1,0:T(1,128)}), f32[8,1,2304]{2,1,0:T(1,128)S(1)}, u32[]{:S(2)}, u32[]{:S(2)}) async-start(f32[8,1,2304]{2,1,0:T(1,128)} %reshape.225), calls=%async_computation | async-start | bytes 147456 | tf_op jit(solution)/shard_map/all_to_all | solution.py:28
  16.8 1.0 slice_bitcast_fusion.1
  17.8 6.4 %all-to-all-done = f32[8,1,2304]{2,1,0:T(1,128)S(1)} async-done(((f32[8,1,2304]{2,1,0:T(1,128)}), f32[8,1,2304]{2,1,0:T(1,128)S(1)}, u32[]{:S(2)}, u32[]{:S(2)}) %all-to-all-start) | async-done | bytes 73760 | tf_op jit(solution)/shard_map/all_to_all | solution.py:28
  25.8 5.9 %all-gather = bf16[96,48]{1,0:T(8,128)(2,1)S(1)} all-gather(bf16[48,48]{1,0:T(8,128)(2,1)S(1)} %reduce_sum.94), channel_id=2, replica_groups=mesh['dp_0'=2,'dp_1'=2,'context'=32,'tensor_0'=2,'tensor_1'=4] {'tensor_0'}, dimensions={0}, use_global_device_ids=true | all-gather | bytes 13824 | tf_op jit(solution)/shard_map/all_gather | solution.py:41
  31.7 11.9 %all-gather.1 = bf16[8,48,48]{2,1,0:T(8,128)(2,1)S(1)} all-gather(bf16[2,48,48]{2,1,0:T(8,128)(2,1)S(1)} %bitcast.335), channel_id=3, replica_groups=mesh['dp_0'=2,'dp_1'=2,'context'=32,'tensor_0'=2,'tensor_1'=4] {'tensor_1'}, dimensions={0}, use_global_device_ids=true | all-gather | bytes 46080 | tf_op jit(solution)/shard_map/all_gather | solution.py:41
  44.8 3.8 collective-permute-start
  49.5 3.8 collective-permute-start.1
  54.3 12.9 %while.34 = (s32[]{:T(128)}, bf16[4,384,1,128]{3,1,2,0:T(8,128)(2,1)S(1)}, bf16[4,384,1,128]{1,3,0,2:T(8,128)(2,1)S(1)}, f32[4,384,1,128]{1,3,2,0:T(8,128)S(1)},...) while((s32[]{:T(128)}, ...), condition=%wide.region_5.6_spmd.clone, body=%wide.region_1.5_spmd.clone.sunk | while | flops 229735296 | bytes 8774289 | solution.py:94
  56.0 0.9 fusion.153
  59.2 0.9 fusion.153
  62.5 0.9 fusion.153
  65.7 0.9 fusion.153
  68.0 1.9 reduce_sum.98
  71.7 15.6 %while.35 = (s32[]{:T(128)}, bf16[4,384,1,128]{3,1,2,0:T(8,128)(2,1)S(1)}, bf16[4,384,1,128]{1,3,0,2:T(8,128)(2,1)S(1)}, f32[4,576,1,128]{3,1,2,0:T(8,128)}, f32...) while((s32[]{:T(128)}, ...), condition=%wide.region_10.11_spmd.clone, body=%wide.region_6.0_spmd.clone.sunk | while | flops 345045888 | bytes 10400389 | solution.py:94
  72.3 1.0 fusion.167
  73.9 1.0 fusion.166
  76.2 1.0 fusion.167
  77.8 1.0 fusion.166
  80.1 1.0 fusion.167
  81.7 1.0 fusion.166
  84.0 1.1 fusion.167
  85.6 1.0 fusion.166
  87.3 1.5 reduce_sum.97
  89.6 14.9 %collective-permute-start.2 = (f32[192,1,128]{0,2,1:T(8,128)}, f32[192,1,128]{0,2,1:T(8,128)}, u32[]{:S(2)}, u32[]{:S(2)}) collective-permute-start(f32[192,1,128]{0,2,1:T(8,128)} %bitcast.26), channel_id=1, source_target_pairs={{0,248},{8,0},{16,8},{24,16},{32,24},{40,32},{48,40},{56,48},{64,5... | collective-permute-start | bytes 294920 | tf_op jit(solution)/shard_map/ppermute | solution.py:55
  104.5 1.4 reduce_sum.100
  106.6 3.9 collective-permute-start.3
  111.5 1.9 fusion.78
  113.8 1.0 fusion.73
  115.1 1.0 fusion.71
  116.5 0.8 reshape.227
  117.3 3.4 all-to-all-start.1
  120.8 0.9 convolution_multiply_fusion.4
  121.7 6.8 %all-to-all-done.1 = f32[8,1,2304]{2,1,0:T(1,128)S(1)} async-done(((f32[8,1,2304]{2,1,0:T(1,128)}), f32[8,1,2304]{2,1,0:T(1,128)S(1)}, u32[]{:S(2)}, u32[]{:S(2)}) %all-to-all-start.1) | async-done | bytes 73760 | tf_op jit(solution)/shard_map/all_to_all | solution.py:28
  129.6 5.9 %all-gather.2 = bf16[96,48]{1,0:T(8,128)(2,1)S(1)} all-gather(bf16[48,48]{1,0:T(8,128)(2,1)S(1)} %copy.96), channel_id=4, replica_groups=mesh['dp_0'=2,'dp_1'=2,'context'=32,'tensor_0'=2,'tensor_1'=4] {'tensor_0'}, dimensions={0}, use_global_device_ids=true | all-gather | bytes 13824 | tf_op jit(solution)/shard_map/all_gather | solution.py:41
  135.5 11.9 %all-gather.3 = bf16[8,48,48]{2,1,0:T(8,128)(2,1)S(1)} all-gather(bf16[2,48,48]{2,1,0:T(8,128)(2,1)S(1)} %bitcast.336), channel_id=5, replica_groups=mesh['dp_0'=2,'dp_1'=2,'context'=32,'tensor_0'=2,'tensor_1'=4] {'tensor_1'}, dimensions={0}, use_global_device_ids=true | all-gather | bytes 46080 | tf_op jit(solution)/shard_map/all_gather | solution.py:41
  147.7 0.9 convolution_bitcast_fusion.8
  148.7 58.3 %all-reduce.13.cloned.1.call-done = (f32[1024,48]{0,1:T(8,128)}, f32[16,1024]{1,0:T(8,128)}) async-done(((f32[1024,48]{0,1:T(8,128)}, f32[16,1024]{1,0:T(8,128)}), (f32[1024,48]{0,1:T(8,128)}, f32[16,1024]{1,0:T(8,128)})) %all-reduce.13.cloned.1.call-update) | async-done | bytes 262160 | tf_op jit(solution)/shard_map/psum | solution.py:59
  207.7 1.2 convert_element_type.115
  209.0 61.1 %all-reduce.11.cloned.1.call-done = (f32[1024,48]{0,1:T(8,128)}, f32[16,1024]{1,0:T(8,128)}) async-done(((f32[1024,48]{0,1:T(8,128)}, f32[16,1024]{1,0:T(8,128)}), (f32[1024,48]{0,1:T(8,128)}, f32[16,1024]{1,0:T(8,128)})) %all-reduce.11.cloned.1.call-update) | async-done | bytes 262160 | tf_op jit(solution)/shard_map/psum | solution.py:59
  270.3 9.7 %psum.69 = f32[2,16,128]{2,1,0:T(8,128)S(1)} all-reduce(f32[2,16,128]{2,1,0:T(8,128)S(1)} %pad_maximum_fusion.3), channel_id=1, replica_groups=mesh['dp_0'=2,'dp_1'=2,'context'=32,'tensor_0'=2,'tensor_1'=4] {'dp_0'}, use_global_device_ids=true, to_apply=%region_22.23 | all-reduce | flops 4096 | bytes 32768 | tf_op jit(solution)/shard_map/psum | solution.py:59
  280.0 3.3 psum.70
  283.3 107.7 %psum.71 = f32[2,16,128]{2,1,0:T(8,128)} all-reduce(f32[2,16,128]{2,1,0:T(8,128)S(1)} %psum.70), channel_id=1, replica_groups=mesh['dp_0'=2,'dp_1'=2,'context'=32,'tensor_0'=2,'tensor_1'=4] {'context'}, use_global_device_ids=true, to_apply=%region_24.25 | all-reduce | flops 4096 | bytes 32768 | tf_op jit(solution)/shard_map/psum | solution.py:59
  391.0 148.4 %all-reduce.9.cloned.1.call-done = (f32[1024,48]{0,1:T(8,128)}, f32[16,1024]{1,0:T(8,128)}) async-done(((f32[1024,48]{0,1:T(8,128)}, f32[16,1024]{1,0:T(8,128)}), (f32[1024,48]{0,1:T(8,128)}, f32[16,1024]{1,0:T(8,128)})) %all-reduce.9.cloned.1.call-update) | async-done | bytes 262160 | tf_op jit(solution)/shard_map/psum | solution.py:59
  539.4 1.6 copy.173
  541.0 1.5 copy.174
  (160 shorter events, 29.3 us)
Async XLA Ops:
  7.2 1.1 copy-start
  7.2 9.2 %copy-start.7 = (bf16[1,384,1024]{2,1,0:T(8,128)(2,1)S(1)}, bf16[1,384,1024]{2,1,0:T(8,128)(2,1)}, u32[]{:S(2)}) copy-start(bf16[1,384,1024]{2,1,0:T(8,128)(2,1)} %param.19) | copy-start | bytes 2359300
  10.4 13.9 %all-to-all-start = ((f32[8,1,2304]{2,1,0:T(1,128)}), f32[8,1,2304]{2,1,0:T(1,128)S(1)}, u32[]{:S(2)}, u32[]{:S(2)}) async-start(f32[8,1,2304]{2,1,0:T(1,128)} %reshape.225), calls=%async_computation | async-start | bytes 147456 | tf_op jit(solution)/shard_map/all_to_all | solution.py:28
  16.8 27.1 %copy-start.15 = (bf16[1,384,128]{2,1,0:T(8,128)(2,1)S(1)}, bf16[1,384,128]{2,1,0:T(8,128)(2,1)}, u32[]{:S(2)}) copy-start(bf16[1,384,128]{2,1,0:T(8,128)(2,1)} %param.14) | copy-start | bytes 294916
  16.8 27.1 %copy-start.17 = (bf16[2,16,128]{2,1,0:T(8,128)(2,1)S(1)}, bf16[2,16,128]{2,1,0:T(8,128)(2,1)}, u32[]{:S(2)}) copy-start(bf16[2,16,128]{2,1,0:T(8,128)(2,1)} %param.18) | copy-start | bytes 24580
  16.8 31.8 %copy-start.16 = (bf16[1,384,128]{2,1,0:T(8,128)(2,1)S(1)}, bf16[1,384,128]{2,1,0:T(8,128)(2,1)}, u32[]{:S(2)}) copy-start(bf16[1,384,128]{2,1,0:T(8,128)(2,1)} %param.15) | copy-start | bytes 294916
  17.8 35.4 %copy-start.8 = (bf16[1,384,1024]{2,1,0:T(8,128)(2,1)S(1)}, bf16[1,384,1024]{2,1,0:T(8,128)(2,1)}, u32[]{:S(2)}) copy-start(bf16[1,384,1024]{2,1,0:T(8,128)(2,1)} %param.13) | copy-start | bytes 2359300
  17.8 35.5 %copy-start.14 = (bf16[16,1024]{1,0:T(8,128)(2,1)S(1)}, bf16[16,1024]{1,0:T(8,128)(2,1)}, u32[]{:S(2)}) copy-start(bf16[16,1024]{1,0:T(8,128)(2,1)} %param.17) | copy-start | bytes 98308
  43.9 10.0 %copy-start.11 = (bf16[384,48]{0,1:T(8,128)(2,1)}, bf16[384,48]{0,1:T(8,128)(2,1)S(1)}, u32[]{:S(2)}) copy-start(bf16[384,48]{0,1:T(8,128)(2,1)S(1)} %reshape_reshape.6) | copy-start | bytes 110596
  44.8 25.2 %collective-permute-start = (bf16[192,1,128]{2,0,1:T(8,128)(2,1)}, bf16[192,1,128]{2,0,1:T(8,128)(2,1)}, u32[]{:S(2)}, u32[]{:S(2)}) collective-permute-start(bf16[192,1,128]{2,0,1:T(8,128)(2,1)} %slice_bitcast_fusion.3), channel_id=1, source_target_pairs={{0,8},{8,16},{16,24},{24,32},{32,40},{40,48},{48,56},{56,64},{64,7... | collective-permute-start | bytes 147464 | tf_op jit(solution)/shard_map/ppermute | solution.py:55
  49.5 21.3 %collective-permute-start.1 = (bf16[192,1,128]{2,0,1:T(8,128)(2,1)}, bf16[192,1,128]{2,0,1:T(8,128)(2,1)}, u32[]{:S(2)}, u32[]{:S(2)}) collective-permute-start(bf16[192,1,128]{2,0,1:T(8,128)(2,1)} %slice_bitcast_fusion.2), channel_id=1, source_target_pairs={{0,8},{8,16},{16,24},{24,32},{32,40},{40,48},{48,56},{56,64},{64,7... | collective-permute-start | bytes 147464 | tf_op jit(solution)/shard_map/ppermute | solution.py:55
  54.3 1.0 copy-start.10
  57.6 1.0 copy-start.10
  60.8 1.0 copy-start.10
  64.0 1.0 copy-start.10
  68.0 3.7 copy-start.9
  87.3 18.5 %copy-start.1 = (bf16[4,384,1,128]{3,1,2,0:T(8,128)(2,1)}, bf16[4,384,1,128]{3,1,2,0:T(8,128)(2,1)S(1)}, u32[]{:S(2)}) copy-start(bf16[4,384,1,128]{3,1,2,0:T(8,128)(2,1)S(1)} %get-tuple-element.115) | copy-start | bytes 1179652
  88.8 21.7 %copy-start.3 = (f32[576,128]{1,0:T(8,128)}, f32[576,128]{1,0:T(8,128)S(1)}, u32[]{:S(2)}) copy-start(f32[576,128]{1,0:T(8,128)S(1)} %reduce_sum.97) | copy-start | bytes 884740
  89.6 24.1 %collective-permute-start.2 = (f32[192,1,128]{0,2,1:T(8,128)}, f32[192,1,128]{0,2,1:T(8,128)}, u32[]{:S(2)}, u32[]{:S(2)}) collective-permute-start(f32[192,1,128]{0,2,1:T(8,128)} %bitcast.26), channel_id=1, source_target_pairs={{0,248},{8,0},{16,8},{24,16},{32,24},{40,32},{48,40},{56,48},{64,5... | collective-permute-start | bytes 294920 | tf_op jit(solution)/shard_map/ppermute | solution.py:55
  105.8 4.7 copy-start.4
  106.6 8.5 %collective-permute-start.3 = (f32[192,1,128]{0,2,1:T(8,128)}, f32[192,1,128]{0,2,1:T(8,128)}, u32[]{:S(2)}, u32[]{:S(2)}) collective-permute-start(f32[192,1,128]{0,2,1:T(8,128)} %bitcast.31), channel_id=1, source_target_pairs={{0,248},{8,0},{16,8},{24,16},{32,24},{40,32},{48,40},{56,48},{64,5... | collective-permute-start | bytes 294920 | tf_op jit(solution)/shard_map/ppermute | solution.py:55
  111.5 2.0 slice-start
  111.5 2.1 slice-start.1
  111.5 2.2 copy-start.6
  113.5 1.7 copy-start.5
  113.6 2.9 copy-start.13
  114.8 6.0 %copy-start.12 = (bf16[384,48]{0,1:T(8,128)(2,1)S(1)}, bf16[384,48]{0,1:T(8,128)(2,1)}, u32[]{:S(2)}) copy-start(bf16[384,48]{0,1:T(8,128)(2,1)} %copy-done.11) | copy-start | bytes 110596
  117.3 11.2 %all-to-all-start.1 = ((f32[8,1,2304]{2,1,0:T(1,128)}), f32[8,1,2304]{2,1,0:T(1,128)S(1)}, u32[]{:S(2)}, u32[]{:S(2)}) async-start(f32[8,1,2304]{2,1,0:T(1,128)} %reshape.227), calls=%async_computation.1 | async-start | bytes 147456 | tf_op jit(solution)/shard_map/all_to_all | solution.py:28
  120.7 86.3 %all-reduce.13.cloned.1.call-start = ((), (), s32[]{:S(2)}) async-start(), calls=%async_computation.4 | async-start | bytes 524288 | tf_op jit(solution)/shard_map/psum | solution.py:59
  129.5 77.6 %copy-start.2 = (bf16[4,384,1,128]{3,1,2,0:T(8,128)(2,1)S(1)}, bf16[4,384,1,128]{3,1,2,0:T(8,128)(2,1)}, u32[]{:S(2)}) copy-start(bf16[4,384,1,128]{3,1,2,0:T(8,128)(2,1)} %copy-done.1) | copy-start | bytes 1179652
  148.6 121.5 %all-reduce.11.cloned.1.call-start = ((), (), s32[]{:S(2)}) async-start(), calls=%async_computation.3 | async-start | bytes 524288 | tf_op jit(solution)/shard_map/psum | solution.py:59
  207.0 332.4 %all-reduce.9.cloned.1.call-start = ((), (), s32[]{:S(2)}) async-start(), calls=%async_computation.2 | async-start | bytes 524288 | tf_op jit(solution)/shard_map/psum | solution.py:59
Sparse Core Ops, SparseCore 0:
  148.7 58.1 all-reduce.12
  210.5 59.6 all-reduce.10
  272.5 266.8 all-reduce.8
where the time goes:
time: 550 us; the launch traced here: 549 us
  waiting for transfers between devices  281 us (51%)
  blocking collectives  156 us (28%)
  starting transfers between devices  35.9 us (7%)
  matrix products  29.6 us (5%)
  local copies, waits for them, and re-layouts  17.6 us (3%)
  between operations  14.3 us (3%)
  other arithmetic  13.8 us (3%)
    psum x3, waiting for transfers between devices, by_axis(): return functools.reduce(lax.psum, axes, shard)  268 us
    psum x3, blocking collectives, by_axis(): return functools.reduce(lax.psum, axes, shard)  121 us
    all_gather x4, blocking collectives, gather_in_order(): tiles = lax.all_gather(tiles, axes[k])  35.6 us
    ppermute x4, starting transfers between devices, shifted(): return lax.ppermute(value, axis, pairs)  26.4 us
    all_to_all x2, waiting for transfers between devices, sent_and_summed(): tiles = lax.all_to_all(cut_along(shard, dim, count), axis, 0, 0, tiled=True)  13.2 us
  transfers between devices with their start and end apart: 9, of which 5 were waited for; matrix products, arithmetic and copies ran while one was open for 5% of the time, Pallas kernels for 0%

commit v1 on v0

--- a/solution.py
+++ b/solution.py
@@ -3,6 +3,8 @@
 import jax
 import jax.numpy as jnp
 from jax import lax
+from jax.experimental import pallas as pl
+from jax.experimental.pallas import tpu as pltpu
 from jax.sharding import Mesh
 from jax.sharding import PartitionSpec as P
 
@@ -53,10 +55,6 @@
     count = lax.axis_size(axis)
     pairs = [(source, (source + steps) % count) for source in range(count)]
     return lax.ppermute(value, axis, pairs)
-
-
-def by_axis(shard, axes):
-    return functools.reduce(lax.psum, axes, shard)
 
 
 def attend_single(query_rows, key_heads, value_heads, grads, allowed):
@@ -102,6 +100,292 @@
 def head_count_total(partial_sum):
     share = sent_and_summed(partial_sum, TENSOR, 0)
     return gathered_by_axis(share.astype(jnp.bfloat16), TENSOR, (0, 1), 0)
+
+
+MESH_ID = pl.DeviceIdType.MESH
+F32 = jnp.float32
+BF16 = jnp.bfloat16
+STEPS = (2, 1, -1, 0)
+FAR = (4, 3, 5, 2, 6, 1, 7)
+
+
+class Place:
+    def __init__(self):
+        self.x = lax.axis_index("dp_0")
+        self.core = lax.axis_index("dp_1")
+        self.z = lax.axis_index("context")
+        self.half = lax.axis_index("tensor_0")
+        self.y = lax.axis_index("tensor_1")
+        self.depth = lax.axis_size("context")
+
+    def near(self, a, b, step):
+        z = lax.rem(self.z + step + self.depth, self.depth)
+        return {
+            "dp_0": lax.rem(self.x + a, 2),
+            "dp_1": lax.rem(self.core + b, 2),
+            "context": z,
+        }
+
+    def along(self, step):
+        return {"context": lax.rem(self.z + step + self.depth, self.depth)}
+
+    def chunk(self, a, b, step):
+        x = lax.rem(self.x + a, 2)
+        core = lax.rem(self.core + b, 2)
+        return (x * 2 + core) * 4 + lax.rem(self.z + step + 4, 4)
+
+
+def near_partners():
+    for step in STEPS:
+        for a in (1, 0):
+            for b in (1, 0):
+                if a or b or step:
+                    yield a, b, step, (a * 2 + b) * 4 + STEPS.index(step)
+
+
+def remote(src, dst, send_sem, recv_sem, device):
+    return pltpu.make_async_remote_copy(
+        src_ref=src,
+        dst_ref=dst,
+        send_sem=send_sem,
+        recv_sem=recv_sem,
+        device_id=device,
+        device_id_type=MESH_ID,
+    )
+
+
+class TensorSum:
+    def __init__(self, place, xs, xr, ys, yr, send, recv):
+        self.xs, self.xr, self.ys, self.yr = xs, xr, ys, yr
+        half = lax.rem(place.half + 1, 2)
+        self.first = remote(xs, xr, send.at[0], recv.at[0], {"tensor_0": half})
+        self.second = [
+            remote(
+                ys,
+                yr.at[k - 1],
+                send.at[k],
+                recv.at[k],
+                {"tensor_1": lax.rem(place.y + k, 4)},
+            )
+            for k in (2, 1, 3)
+        ]
+
+    def start(self, part):
+        self.part = part
+        self.xs[...] = part.astype(BF16)
+        self.first.start()
+
+    def middle(self):
+        self.first.wait()
+        self.total = self.part + self.xr[...].astype(F32)
+        self.ys[...] = self.total.astype(BF16)
+        for copy in self.second:
+            copy.start()
+
+    def end(self):
+        for copy in self.second:
+            copy.wait()
+        total = self.total
+        for k in range(3):
+            total = total + self.yr[k].astype(F32)
+        return total
+
+
+class TokenSum:
+    def __init__(self, place, mine, got, spread, full, send, recv):
+        self.place = place
+        self.mine, self.got, self.spread, self.full = mine, got, spread, full
+        own = place.chunk(0, 0, 0)
+        self.own = own
+        self.group = place.z // 4
+        groups = place.depth // 4
+        self.first, self.third = [], []
+        for a, b, step, slot in near_partners():
+            device = place.near(a, b, step)
+            self.first.append(
+                (
+                    slot,
+                    remote(
+                        mine.at[place.chunk(a, b, step)],
+                        got.at[slot],
+                        send.at[slot],
+                        recv.at[slot],
+                        device,
+                    ),
+                )
+            )
+            self.third.append(
+                remote(
+                    full.at[own], full.at[own], send.at[24 + slot], recv.at[24 + slot], device
+                )
+            )
+        self.second = [
+            remote(
+                spread.at[self.group],
+                spread.at[self.group],
+                send.at[16 + k],
+                recv.at[16 + k],
+                place.along(4 * k),
+            )
+            for k in FAR
+        ]
+        self.groups = groups
+
+    def start(self):
+        for _, copy in self.first:
+            copy.start()
+
+    def middle(self):
+        total = self.mine[self.own].astype(F32)
+        for slot, copy in self.first:
+            copy.wait_recv()
+            total = total + self.got[slot].astype(F32)
+        self.spread[self.group] = total.astype(BF16)
+        for copy in self.second:
+            copy.start()
+
+    def late(self):
+        for copy in self.second:
+            copy.wait_recv()
+        total = self.spread[0].astype(F32)
+        for k in range(1, 8):
+            total = total + self.spread[k].astype(F32)
+        self.full[self.own] = total.astype(BF16)
+        for copy in self.third:
+            copy.start()
+
+    def end(self):
+        for copy in self.third:
+            copy.wait_recv()
+
+    def drain(self):
+        for _, copy in self.first:
+            copy.wait_send()
+        for copy in self.second:
+            copy.wait_send()
+        for copy in self.third:
+            copy.wait_send()
+
+
+def greet(place):
+    barrier = pltpu.get_barrier_semaphore()
+    partners = []
+    for step in (2, -2, 1, -1, 0):
+        for a in (1, 0):
+            for b in (1, 0):
+                if a or b or step:
+                    partners.append(place.near(a, b, step))
+    for k in FAR:
+        partners.append(place.along(4 * k))
+    partners.append({"tensor_0": lax.rem(place.half + 1, 2)})
+    for k in (2, 1, 3):
+        partners.append({"tensor_1": lax.rem(place.y + k, 4)})
+    for device in partners:
+        pl.semaphore_signal(barrier, inc=1, device_id=device, device_id_type=MESH_ID)
+    pl.semaphore_wait(barrier, len(partners))
+
+
+def tail_kernel(
+    part_ref,
+    normed_ref,
+    up_ref,
+    pair_ref,
+    down_out,
+    up_out,
+    pair_out,
+    xs,
+    xr,
+    ys,
+    yr,
+    tsend,
+    trecv,
+    e_mine,
+    e_got,
+    e_spread,
+    e_full,
+    esend,
+    erecv,
+    g_mine,
+    g_got,
+    g_spread,
+    g_full,
+    gsend,
+    grecv,
+):
+    place = Place()
+    greet(place)
+    early = TokenSum(place, e_mine, e_got, e_spread, e_full, esend, erecv)
+    late = TokenSum(place, g_mine, g_got, g_spread, g_full, gsend, grecv)
+    ranks = TensorSum(place, xs, xr, ys, yr, tsend, trecv)
+    ranks.start(part_ref[...])
+    zeros = jnp.zeros((8, 128), F32)
+    for c in range(16):
+        top = up_ref[8 * (c % 2) : 8 * (c % 2) + 8, 128 * (c // 2) : 128 * (c // 2) + 128]
+        low = pair_ref[8 * c : 8 * c + 8, :] if c < 4 else zeros
+        e_mine[c] = jnp.concatenate([top, low], axis=0).astype(BF16)
+    early.start()
+    ranks.middle()
+    early.middle()
+    rank_grad = (adapter_scale * ranks.end()).astype(BF16)
+    for j in range(8):
+        columns = slice(128 * j, 128 * j + 128)
+        down = jnp.dot(rank_grad, normed_ref[:, columns], preferred_element_type=F32)
+        g_mine[2 * j] = down[:24].astype(BF16)
+        g_mine[2 * j + 1] = down[24:].astype(BF16)
+    late.start()
+    late.middle()
+    early.late()
+    early.end()
+    for c in range(16):
+        value = e_full[c].astype(F32)
+        up_out[8 * (c % 2) : 8 * (c % 2) + 8, 128 * (c // 2) : 128 * (c // 2) + 128] = value[:8]
+        if c < 4:
+            pair_out[8 * c : 8 * c + 8, :] = value[8:]
+    late.late()
+    late.end()
+    for c in range(16):
+        down_out[24 * (c % 2) : 24 * (c % 2) + 24, 128 * (c // 2) : 128 * (c // 2) + 128] = g_full[
+            c
+        ].astype(F32)
+    early.drain()
+    late.drain()
+
+
+def token_sum_scratch(rows):
+    return [
+        pltpu.VMEM((16, rows, 128), BF16),
+        pltpu.VMEM((16, rows, 128), BF16),
+        pltpu.VMEM((8, rows, 128), BF16),
+        pltpu.VMEM((16, rows, 128), BF16),
+        pltpu.SemaphoreType.DMA((40,)),
+        pltpu.SemaphoreType.DMA((40,)),
+    ]
+
+
+def tail(part, normed, up, pair):
+    vmem = pl.BlockSpec(memory_space=pltpu.VMEM)
+    ranks, tokens = part.shape
+    return pl.pallas_call(
+        tail_kernel,
+        out_shape=(
+            jax.ShapeDtypeStruct((ranks, normed.shape[1]), F32),
+            jax.ShapeDtypeStruct(up.shape, F32),
+            jax.ShapeDtypeStruct(pair.shape, F32),
+        ),
+        in_specs=[vmem] * 4,
+        out_specs=(vmem,) * 3,
+        scratch_shapes=[
+            pltpu.VMEM((ranks, tokens), BF16),
+            pltpu.VMEM((ranks, tokens), BF16),
+            pltpu.VMEM((ranks, tokens), BF16),
+            pltpu.VMEM((3, ranks, tokens), BF16),
+            pltpu.SemaphoreType.DMA((4,)),
+            pltpu.SemaphoreType.DMA((4,)),
+        ]
+        + token_sum_scratch(16)
+        + token_sum_scratch(24),
+        compiler_params=pltpu.CompilerParams(collective_id=0, has_side_effects=True),
+    )(part, normed, up, pair)
 
 
 def on_device(
@@ -211,36 +495,26 @@
         preferred_element_type=jnp.float32,
     )
     inner_product = (((1,), (1,)), ((), ()))
-    adapter_depth_terms = adapter_scale * jnp.concatenate(
+    outer = (((1,), (1,)), ((), ()))
+    part = jnp.concatenate(
         [
+            lax.dot_general(query_up_weight, query_gradient, outer, preferred_element_type=F32),
             lax.dot_general(
-                query_gradient, query_up_weight, inner_product, preferred_element_type=jnp.float32
+                key_value_up_weight[0], key_gradient, outer, preferred_element_type=F32
             ),
             lax.dot_general(
-                key_gradient,
-                key_value_up_weight[0],
-                inner_product,
-                preferred_element_type=jnp.float32,
-            ),
-            lax.dot_general(
-                value_gradient,
-                key_value_up_weight[1],
-                inner_product,
-                preferred_element_type=jnp.float32,
+                key_value_up_weight[1], value_gradient, outer, preferred_element_type=F32
             ),
         ],
-        axis=1,
-    )
-    reduced_projection_gradient = head_count_total(adapter_depth_terms)
-    grad_down = lax.dot_general(
-        token_count, reduced_projection_gradient, spanning_axis, preferred_element_type=jnp.float32
-    )
-    grad_a, query_up_gradient, grad_bkv = (
-        by_axis(grad_down, DP_CONTEXT),
-        by_axis(query_adapter_gradient, DP_CONTEXT),
-        by_axis(jnp.stack([key_adapter_gradient, value_adapter_gradient]), DP_CONTEXT),
-    )
-    return (attended[None], grad_a, query_up_gradient, grad_bkv)
+        axis=0,
+    )
+    down, up, pair = tail(
+        part,
+        token_count,
+        query_adapter_gradient,
+        jnp.concatenate([key_adapter_gradient, value_adapter_gradient], axis=0),
+    )
+    return (attended[None], down.T, up, pair.reshape(2, adapter_depth, -1))
 
 
 def solution(mesh):

time: 550 us -> 161 us (0.29)
  the two profiles are of different devices: /device:TPU:2 before, /device:TPU:1 now
where the time goes in v1:
time: 161 us; the launch traced here: 160 us
  Pallas kernels  50.2 us (31%)
  starting transfers between devices  32.9 us (20%)
  matrix products  26.7 us (17%)
  local copies, waits for them, and re-layouts  17 us (11%)
  blocking collectives  13.9 us (9%)
  other arithmetic  12 us (7%)
  waiting for transfers between devices  5.43 us (3%)
    pallas_call x1, Pallas kernels, tail(): pl.pallas_call(tail_kernel, out_shape=(jax.ShapeDtypeStruct((ranks, norme...  50.2 us
    ppermute x4, starting transfers between devices, shifted(): return lax.ppermute(value, axis, pairs)  25.4 us
    all_gather x2, blocking collectives, gather_in_order(): tiles = lax.all_gather(tiles, axes[k])  13.9 us
    unnamed x41, local copies, waits for them, and re-layouts  7.81 us
    dot_general x8, matrix products, attend_single(): jnp.einsum('gtu,tgd->ugd', probs_low, grads, preferred_element_type=jnp.f...  7.73 us
    all_to_all x1, starting transfers between devices, sent_and_summed(): tiles = lax.all_to_all(cut_along(shard, dim, count), axis, 0, 0, tiled=True)  7.47 us
    all_to_all x1, waiting for transfers between devices, sent_and_summed(): tiles = lax.all_to_all(cut_along(shard, dim, count), axis, 0, 0, tiled=True)  5.3 us
    dot_general x8, matrix products, attend_single(): jnp.einsum('gtu,tgd->ugd', score_grad, query_rows, preferred_element_type...  4.9 us
  transfers between devices with their start and end apart: 5, of which 2 were waited for; matrix products, arithmetic and copies ran while one was open for 14% of the time, Pallas kernels for 0%

profile of v1, /device:TPU:1, one launch (start us, length us, event | category | flops | bytes accessed | tf_op | source)
XLA Modules:
  0.0 159.8 jit_solution(6923132582577132831)
XLA Ops:
  0.7 0.9 copy-done
  1.5 1.5 fusion.73
  3.0 0.8 reshape.205
  3.8 7.5 %all-to-all-start = ((f32[8,1,2304]{2,1,0:T(1,128)}), f32[8,1,2304]{2,1,0:T(1,128)S(1)}, u32[]{:S(2)}, u32[]{:S(2)}) async-start(f32[8,1,2304]{2,1,0:T(1,128)} %reshape.205), calls=%async_computation | async-start | bytes 147456 | tf_op jit(solution)/shard_map/all_to_all | solution.py:30
  11.7 1.0 slice_bitcast_fusion.1
  12.7 5.3 %all-to-all-done = f32[8,1,2304]{2,1,0:T(1,128)S(1)} async-done(((f32[8,1,2304]{2,1,0:T(1,128)}), f32[8,1,2304]{2,1,0:T(1,128)S(1)}, u32[]{:S(2)}, u32[]{:S(2)}) %all-to-all-start) | async-done | bytes 73760 | tf_op jit(solution)/shard_map/all_to_all | solution.py:30
  18.0 0.5 broadcast.73
  18.5 0.8 reduce.16
  19.5 4.7 %all-gather = bf16[96,48]{1,0:T(8,128)(2,1)S(1)} all-gather(bf16[48,48]{1,0:T(8,128)(2,1)S(1)} %reduce_sum.85), channel_id=2, replica_groups=mesh['dp_0'=2,'dp_1'=2,'context'=32,'tensor_0'=2,'tensor_1'=4] {'tensor_0'}, dimensions={0}, use_global_device_ids=true | all-gather | bytes 13824 | tf_op jit(solution)/shard_map/all_gather | solution.py:43
  24.3 9.2 %all-gather.1 = bf16[8,48,48]{2,1,0:T(8,128)(2,1)S(1)} all-gather(bf16[2,48,48]{2,1,0:T(8,128)(2,1)S(1)} %bitcast.328), channel_id=3, replica_groups=mesh['dp_0'=2,'dp_1'=2,'context'=32,'tensor_0'=2,'tensor_1'=4] {'tensor_1'}, dimensions={0}, use_global_device_ids=true | all-gather | bytes 46080 | tf_op jit(solution)/shard_map/all_gather | solution.py:43
  34.0 3.4 %collective-permute-start = (bf16[192,1,128]{2,0,1:T(8,128)(2,1)S(1)}, bf16[192,1,128]{2,0,1:T(8,128)(2,1)}, u32[]{:S(2)}, u32[]{:S(2)}) collective-permute-start(bf16[192,1,128]{2,0,1:T(8,128)(2,1)S(1)} %slice_bitcast_fusion.3), channel_id=1, source_target_pairs={{0,8},{8,16},{16,24},{24,32},{32,40},{40,48},{48,56},{56,64},{64,7... | collective-permute-start | bytes 147464 | tf_op jit(solution)/shard_map/ppermute | solution.py:57
  37.6 0.6 slice_bitcast_fusion.2
  38.2 3.5 %collective-permute-start.1 = (bf16[192,1,128]{2,0,1:T(8,128)(2,1)}, bf16[192,1,128]{2,0,1:T(8,128)(2,1)S(1)}, u32[]{:S(2)}, u32[]{:S(2)}) collective-permute-start(bf16[192,1,128]{2,0,1:T(8,128)(2,1)} %slice_bitcast_fusion.2), channel_id=1, source_target_pairs={{0,8},{8,16},{16,24},{24,32},{32,40},{40,48},{48,56},{56,64},{64,7... | collective-permute-start | bytes 147464 | tf_op jit(solution)/shard_map/ppermute | solution.py:57
  42.8 15.6 %while.34 = (s32[]{:T(128)}, bf16[4,384,1,128]{3,1,2,0:T(8,128)(2,1)S(1)}, bf16[4,384,1,128]{1,3,0,2:T(8,128)(2,1)S(1)}, f32[4,384,1,128]{1,3,2,0:T(8,128)}, f32...) while((s32[]{:T(128)}, ...), condition=%wide.region_5.6_spmd.clone, body=%wide.region_1.5_spmd.clone.sunk | while | flops 229735296 | bytes 8774289 | solution.py:92
  43.2 0.6 copy-done.8
  44.3 0.9 fusion.146
  45.2 0.9 fusion.147
  47.1 0.6 copy-done.8
  48.2 0.9 fusion.146
  49.1 0.9 fusion.147
  51.1 0.6 copy-done.8
  52.1 0.9 fusion.146
  53.0 0.9 fusion.147
  55.0 0.6 copy-done.8
  56.0 0.9 fusion.146
  56.9 0.9 fusion.147
  58.5 1.9 %reduce_sum.86 = f32[384,128]{0,1:T(8,128)} reduce(f32[4,384,1,128]{1,3,2,0:T(8,128)} %get-tuple-element.121, f32[]{:T(128)} %constant.49.clone.1), dimensions={0,2}, to_apply=%region_11.12 | reduce | flops 147456 | bytes 983044 | tf_op jit(solution)/shard_map/reduce_sum | solution.py:95
  60.4 1.9 %reduce_sum.89 = f32[384,128]{0,1:T(8,128)} reduce(f32[4,384,1,128]{1,3,2,0:T(8,128)} %get-tuple-element.123, f32[]{:T(128)} %constant.49.clone.1), dimensions={0,2}, to_apply=%region_13.14 | reduce | flops 147456 | bytes 983044 | tf_op jit(solution)/shard_map/reduce_sum | solution.py:96
  62.2 0.8 pad_maximum_fusion.2
  63.1 0.7 pad_maximum_fusion.3
  63.8 14.3 %while.35 = (s32[]{:T(128)}, bf16[4,384,1,128]{3,1,2,0:T(8,128)(2,1)S(1)}, bf16[4,384,1,128]{1,3,0,2:T(8,128)(2,1)S(1)}, f32[4,576,1,128]{3,1,2,0:T(8,128)S(1)},...) while((s32[]{:T(128)}, ...), condition=%wide.region_10.11_spmd.clone, body=%wide.region_6.0_spmd.clone.sunk | while | flops 345045888 | bytes 12563133 | solution.py:92
  64.8 1.0 fusion.161
  68.4 1.0 fusion.161
  72.0 1.0 fusion.161
  75.6 1.0 fusion.161
  78.2 1.5 reduce_sum.91
  79.7 0.7 slice.100
  81.2 0.9 convolution_multiply_fusion.4.up_ref
  82.4 15.1 %collective-permute-start.2 = (f32[192,1,128]{0,2,1:T(8,128)S(1)}, f32[192,1,128]{0,2,1:T(8,128)S(1)}, u32[]{:S(2)}, u32[]{:S(2)}) collective-permute-start(f32[192,1,128]{0,2,1:T(8,128)S(1)} %bitcast.327), channel_id=1, source_target_pairs={{0,248},{8,0},{16,8},{24,16},{32,24},{40,32},{48,40},{56,48},{64,5... | collective-permute-start | bytes 294920 | tf_op jit(solution)/shard_map/ppermute | solution.py:57
  97.8 3.4 %collective-permute-start.3 = (f32[192,1,128]{0,2,1:T(8,128)S(1)}, f32[192,1,128]{0,2,1:T(8,128)S(1)}, u32[]{:S(2)}, u32[]{:S(2)}) collective-permute-start(f32[192,1,128]{0,2,1:T(8,128)S(1)} %bitcast.326), channel_id=1, source_target_pairs={{0,248},{8,0},{16,8},{24,16},{32,24},{40,32},{48,40},{56,48},{64,5... | collective-permute-start | bytes 294920 | tf_op jit(solution)/shard_map/ppermute | solution.py:57
  101.3 0.5 copy.61
  101.8 1.2 convert_element_type.96
  103.9 0.6 pad_maximum_fusion.5.pair_ref
  104.5 0.6 pad_maximum_fusion.4.part_ref
  105.1 50.2 %shard_map.111 = (f32[48,1024]{1,0:T(8,128)}, f32[16,1024]{1,0:T(8,128)}, f32[32,128]{1,0:T(8,128)}) custom-call(f32[48,384]{1,0:T(8,128)} %pad_maximum_fusion.4.part_ref, bf16[384,1024]{1,0:T(8,128)(2,1)} %bitcast.314, f32[16,1024]{1,0:T(8,128)} %convolution_multiply_fusion.4.up_ref, f32[32,128]{1,0:T(8,128)} %pad_maximum_fusion.5.pair_ref), custom_call_target="tpu_custom_call" | custom-call | tf_op jit(solution)/shard_map/pallas_call | solution.py:368
  155.3 1.6 %copy.139 = f32[1024,48]{0,1:T(8,128)} copy(f32[1024,48]{0,1:T(8,128)} %bitcast.325) | data formatting | bytes 393216
  157.0 1.5 copy.140
  158.4 1.3 copy.141
  (144 shorter events, 20.2 us)
Async XLA Ops:
  0.6 0.9 copy-start
  0.6 10.7 %copy-start.4 = (bf16[1,384,1024]{2,1,0:T(8,128)(2,1)S(1)}, bf16[1,384,1024]{2,1,0:T(8,128)(2,1)}, u32[]{:S(2)}) copy-start(bf16[1,384,1024]{2,1,0:T(8,128)(2,1)} %param.19) | copy-start | bytes 2359300
  3.8 14.2 %all-to-all-start = ((f32[8,1,2304]{2,1,0:T(1,128)}), f32[8,1,2304]{2,1,0:T(1,128)S(1)}, u32[]{:S(2)}, u32[]{:S(2)}) async-start(f32[8,1,2304]{2,1,0:T(1,128)} %reshape.205), calls=%async_computation | async-start | bytes 147456 | tf_op jit(solution)/shard_map/all_to_all | solution.py:30
  11.7 22.0 %copy-start.14 = (bf16[1,384,128]{2,1,0:T(8,128)(2,1)S(1)}, bf16[1,384,128]{2,1,0:T(8,128)(2,1)}, u32[]{:S(2)}) copy-start(bf16[1,384,128]{2,1,0:T(8,128)(2,1)} %param.14) | copy-start | bytes 294916
  11.7 22.0 %copy-start.16 = (bf16[2,16,128]{2,1,0:T(8,128)(2,1)S(1)}, bf16[2,16,128]{2,1,0:T(8,128)(2,1)}, u32[]{:S(2)}) copy-start(bf16[2,16,128]{2,1,0:T(8,128)(2,1)} %param.18) | copy-start | bytes 24580
  11.7 25.7 %copy-start.15 = (bf16[1,384,128]{2,1,0:T(8,128)(2,1)S(1)}, bf16[1,384,128]{2,1,0:T(8,128)(2,1)}, u32[]{:S(2)}) copy-start(bf16[1,384,128]{2,1,0:T(8,128)(2,1)} %param.15) | copy-start | bytes 294916
  12.7 29.1 %copy-start.5 = (bf16[1,384,1024]{2,1,0:T(8,128)(2,1)S(1)}, bf16[1,384,1024]{2,1,0:T(8,128)(2,1)}, u32[]{:S(2)}) copy-start(bf16[1,384,1024]{2,1,0:T(8,128)(2,1)} %param.13) | copy-start | bytes 2359300
  12.7 29.1 %copy-start.12 = (bf16[16,1024]{1,0:T(8,128)(2,1)S(1)}, bf16[16,1024]{1,0:T(8,128)(2,1)}, u32[]{:S(2)}) copy-start(bf16[16,1024]{1,0:T(8,128)(2,1)} %param.17) | copy-start | bytes 98308
  33.7 8.7 %copy-start.9 = (bf16[384,48]{0,1:T(8,128)(2,1)}, bf16[384,48]{0,1:T(8,128)(2,1)S(1)}, u32[]{:S(2)}) copy-start(bf16[384,48]{0,1:T(8,128)(2,1)S(1)} %reshape_reshape.3) | copy-start | bytes 110596
  34.0 28.2 %collective-permute-start = (bf16[192,1,128]{2,0,1:T(8,128)(2,1)S(1)}, bf16[192,1,128]{2,0,1:T(8,128)(2,1)}, u32[]{:S(2)}, u32[]{:S(2)}) collective-permute-start(bf16[192,1,128]{2,0,1:T(8,128)(2,1)S(1)} %slice_bitcast_fusion.3), channel_id=1, source_target_pairs={{0,8},{8,16},{16,24},{24,32},{32,40},{40,48},{48,56},{56,64},{64,7... | collective-permute-start | bytes 147464 | tf_op jit(solution)/shard_map/ppermute | solution.py:57
  38.2 24.8 %collective-permute-start.1 = (bf16[192,1,128]{2,0,1:T(8,128)(2,1)}, bf16[192,1,128]{2,0,1:T(8,128)(2,1)S(1)}, u32[]{:S(2)}, u32[]{:S(2)}) collective-permute-start(bf16[192,1,128]{2,0,1:T(8,128)(2,1)} %slice_bitcast_fusion.2), channel_id=1, source_target_pairs={{0,8},{8,16},{16,24},{24,32},{32,40},{40,48},{48,56},{56,64},{64,7... | collective-permute-start | bytes 147464 | tf_op jit(solution)/shard_map/ppermute | solution.py:57
  42.8 1.0 copy-start.8
  46.7 1.0 copy-start.8
  50.7 1.0 copy-start.8
  54.6 1.0 copy-start.8
  63.8 1.0 copy-start.7
  64.8 1.0 copy-start.11
  67.4 1.0 copy-start.7
  68.4 1.0 copy-start.11
  71.0 1.0 copy-start.7
  72.0 1.0 copy-start.11
  74.6 1.0 copy-start.7
  75.6 1.0 copy-start.11
  78.2 2.2 %copy-start.1 = (f32[576,128]{1,0:T(8,128)}, f32[576,128]{1,0:T(8,128)S(1)}, u32[]{:S(2)}) copy-start(f32[576,128]{1,0:T(8,128)S(1)} %reduce_sum.88) | copy-start | bytes 884740
  79.7 0.9 copy-start.13
  80.4 0.8 copy-start.10
  80.5 1.6 %slice-start = ((f32[576,128]{1,0:T(8,128)}), f32[384,128]{1,0:T(8,128)S(1)}, s32[]{:S(2)}) async-start(f32[576,128]{1,0:T(8,128)} %copy-done.1), calls=%async_computation.1 | async-start | bytes 393216 | tf_op jit(solution)/shard_map/slice | solution.py:466
  80.6 1.7 %slice-start.1 = ((f32[576,128]{1,0:T(8,128)}), f32[192,128]{1,0:T(8,128)S(1)}, s32[]{:S(2)}) async-start(f32[576,128]{1,0:T(8,128)} %copy-done.1), calls=%async_computation.2 | async-start | bytes 196608 | tf_op jit(solution)/shard_map/slice | solution.py:462
  80.6 17.0 %copy-start.6 = (f32[384,128]{1,0:T(8,128)S(1)}, f32[384,128]{1,0:T(8,128)}, u32[]{:S(2)}) copy-start(f32[384,128]{1,0:T(8,128)} %slice.100) | copy-start | bytes 589828
  82.4 20.6 %collective-permute-start.2 = (f32[192,1,128]{0,2,1:T(8,128)S(1)}, f32[192,1,128]{0,2,1:T(8,128)S(1)}, u32[]{:S(2)}, u32[]{:S(2)}) collective-permute-start(f32[192,1,128]{0,2,1:T(8,128)S(1)} %bitcast.327), channel_id=1, source_target_pairs={{0,248},{8,0},{16,8},{24,16},{32,24},{40,32},{48,40},{56,48},{64,5... | collective-permute-start | bytes 294920 | tf_op jit(solution)/shard_map/ppermute | solution.py:57
  97.8 5.7 %collective-permute-start.3 = (f32[192,1,128]{0,2,1:T(8,128)S(1)}, f32[192,1,128]{0,2,1:T(8,128)S(1)}, u32[]{:S(2)}, u32[]{:S(2)}) collective-permute-start(f32[192,1,128]{0,2,1:T(8,128)S(1)} %bitcast.326), channel_id=1, source_target_pairs={{0,248},{8,0},{16,8},{24,16},{32,24},{40,32},{48,40},{56,48},{64,5... | collective-permute-start | bytes 294920 | tf_op jit(solution)/shard_map/ppermute | solution.py:57
  101.8 1.2 copy-start.3
  101.8 1.7 %copy-start.2 = (f32[384,128]{0,1:T(8,128)S(1)}, f32[384,128]{0,1:T(8,128)}, u32[]{:S(2)}) copy-start(f32[384,128]{0,1:T(8,128)} %reduce_sum.89) | copy-start | bytes 589828

commit v2 on v1

v2 whole, which is shorter than its diff:
```python
import jax
import jax.numpy as jnp
from jax import lax
from jax.experimental import pallas as pl
from jax.experimental.pallas import tpu as pltpu
from jax.sharding import Mesh
from jax.sharding import PartitionSpec as P

HEAD_SIZE = 128
TENSOR = ("tensor_0", "tensor_1")
DP = ("dp_0", "dp_1")
SCALE = HEAD_SIZE**-0.5
LOG2E = 1.4426950408889634
adapter_scale = 2.0

MESH_ID = pl.DeviceIdType.MESH
F32 = jnp.float32
BF16 = jnp.bfloat16
STEPS = (2, 1, -1, 0)
FAR = (4, 3, 5, 2, 6, 1, 7)


class Place:
    def __init__(self):
        self.x = lax.axis_index("dp_0")
        self.core = lax.axis_index("dp_1")
        self.z = lax.axis_index("context")
        self.half = lax.axis_index("tensor_0")
        self.y = lax.axis_index("tensor_1")
        self.depth = lax.axis_size("context")

    def near(self, a, b, step):
        z = lax.rem(self.z + step + self.depth, self.depth)
        return {
            "dp_0": lax.rem(self.x + a, 2),
            "dp_1": lax.rem(self.core + b, 2),
            "context": z,
        }

    def along(self, step):
        return {"context": lax.rem(self.z + step + self.depth, self.depth)}

    def chunk(self, a, b, step):
        x = lax.rem(self.x + a, 2)
        core = lax.rem(self.core + b, 2)
        return (x * 2 + core) * 4 + lax.rem(self.z + step + 4, 4)


def near_partners():
    for step in STEPS:
        for a in (1, 0):
            for b in (1, 0):
                if a or b or step:
                    yield a, b, step, (a * 2 + b) * 4 + STEPS.index(step)


def remote(src, dst, send_sem, recv_sem, device):
    return pltpu.make_async_remote_copy(
        src_ref=src,
        dst_ref=dst,
        send_sem=send_sem,
        recv_sem=recv_sem,
        device_id=device,
        device_id_type=MESH_ID,
    )


class TensorSum:
    def __init__(self, place, xs, xr, ys, yr, send, recv):
        self.xs, self.xr, self.ys, self.yr = xs, xr, ys, yr
        half = lax.rem(place.half + 1, 2)
        self.first = remote(xs, xr, send.at[0], recv.at[0], {"tensor_0": half})
        self.second = [
            remote(
                ys,
                yr.at[k - 1],
                send.at[k],
                recv.at[k],
                {"tensor_1": lax.rem(place.y + k, 4)},
            )
            for k in (2, 1, 3)
        ]

    def start(self, part):
        self.part = part
        self.xs[...] = part.astype(BF16)
        self.first.start()

    def middle(self):
        self.first.wait()
        self.total = self.part + self.xr[...].astype(F32)
        self.ys[...] = self.total.astype(BF16)
        for copy in self.second:
            copy.start()

    def end(self):
        for copy in self.second:
            copy.wait()
        total = self.total
        for k in range(3):
            total = total + self.yr[k].astype(F32)
        return total


class TokenSum:
    def __init__(self, place, mine, got, spread, full, send, recv):
        self.place = place
        self.mine, self.got, self.spread, self.full = mine, got, spread, full
        own = place.chunk(0, 0, 0)
        self.own = own
        self.group = place.z // 4
        groups = place.depth // 4
        self.first, self.third = [], []
        for a, b, step, slot in near_partners():
            device = place.near(a, b, step)
            self.first.append(
                (
                    slot,
                    remote(
                        mine.at[place.chunk(a, b, step)],
                        got.at[slot],
                        send.at[slot],
                        recv.at[slot],
                        device,
                    ),
                )
            )
            self.third.append(
                remote(
                    full.at[own], full.at[own], send.at[24 + slot], recv.at[24 + slot], device
                )
            )
        self.second = [
            remote(
                spread.at[self.group],
                spread.at[self.group],
                send.at[16 + k],
                recv.at[16 + k],
                place.along(4 * k),
            )
            for k in FAR
        ]
        self.groups = groups

    def start(self):
        for _, copy in self.first:
            copy.start()

    def middle(self):
        total = self.mine[self.own].astype(F32)
        for slot, copy in self.first:
            copy.wait_recv()
            total = total + self.got[slot].astype(F32)
        self.spread[self.group] = total.astype(BF16)
        for copy in self.second:
            copy.start()

    def late(self):
        for copy in self.second:
            copy.wait_recv()
        total = self.spread[0].astype(F32)
        for k in range(1, 8):
            total = total + self.spread[k].astype(F32)
        self.full[self.own] = total.astype(BF16)
        for copy in self.third:
            copy.start()

    def end(self):
        for copy in self.third:
            copy.wait_recv()

    def drain(self):
        for _, copy in self.first:
            copy.wait_send()
        for copy in self.second:
            copy.wait_send()
        for copy in self.third:
            copy.wait_send()


NN = (((1,), (0,)), ((), ()))
NT = (((1,), (1,)), ((), ()))
TN = (((0,), (0,)), ((), ()))


def mul(a, b, dims=NN):
    return lax.dot_general(a, b, dims, preferred_element_type=F32)


def greet(place):
    barrier = pltpu.get_barrier_semaphore()
    partners = []
    for step in (2, -2, 1, -1, 0):
        for a in (1, 0):
            for b in (1, 0):
                if a or b or step:
                    partners.append(place.near(a, b, step))
    partners.append({"tensor_0": lax.rem(place.half + 1, 2)})
    for k in (2, 1, 3):
        partners.append({"tensor_1": lax.rem(place.y + k, 4)})
    for device in partners:
        pl.semaphore_signal(barrier, inc=1, device_id=device, device_id_type=MESH_ID)
    return barrier, len(partners)


def tell(place, sem, step):
    for device in (place.along(step), place.along(-step)):
        pl.semaphore_signal(sem, inc=1, device_id=device, device_id_type=MESH_ID)


def kernel(
    normed_hbm,
    query_hbm,
    key_ref,
    value_ref,
    down_ref,
    up_ref,
    pair_ref,
    grad_hbm,
    attended_hbm,
    down_out,
    up_out,
    pair_out,
    normed,
    qs,
    dos,
    outs,
    kv,
    dkv,
    bias,
    rank_acc,
    up_acc,
    back_s,
    back_r,
    load_sem,
    store_sem,
    move_send,
    move_recv,
    reach,
    a_xs,
    a_xr,
    a_ys,
    a_yr,
    a_send,
    a_recv,
    d_xs,
    d_xr,
    d_ys,
    d_yr,
    d_send,
    d_recv,
    e_mine,
    e_got,
    e_spread,
    e_full,
    esend,
    erecv,
    g_mine,
    g_got,
    g_spread,
    g_full,
    gsend,
    grecv,
):
    place = Place()
    tokens = normed.shape[0]
    half = tokens // 2
    depth = up_ref.shape[0]
    heads = up_ref.shape[1] // HEAD_SIZE

    load = pltpu.make_async_copy(normed_hbm, normed, load_sem.at[0])
    load.start()
    loads = []
    for source, target, first in ((query_hbm, qs, 1), (grad_hbm, dos, 1 + 2 * heads)):
        for h in range(heads):
            for part in range(2):
                copy = pltpu.make_async_copy(
                    source.at[pl.ds(part * half, half), pl.ds(h * HEAD_SIZE, HEAD_SIZE)],
                    target.at[part, pl.ds(h * half, half), :],
                    load_sem.at[first + 2 * h + part],
                )
                copy.start()
                loads.append(copy)
    barrier, partners = greet(place)

    key_ids = lax.broadcasted_iota(jnp.int32, (half, tokens), 0)
    lanes = lax.broadcasted_iota(jnp.int32, (half, tokens), 1)
    row_ids = jnp.where(lanes < half, lanes, lanes - half)
    bias[...] = jnp.where(key_ids <= row_ids, 0.0, -jnp.inf)
    dkv[...] = jnp.zeros_like(dkv)
    rank_acc[...] = jnp.zeros_like(rank_acc)
    up_acc[...] = jnp.zeros_like(up_acc)

    early = TokenSum(place, e_mine, e_got, e_spread, e_full, esend, erecv)
    late = TokenSum(place, g_mine, g_got, g_spread, g_full, gsend, grecv)
    ranks = TensorSum(place, a_xs, a_xr, a_ys, a_yr, a_send, a_recv)
    rank_grads = TensorSum(place, d_xs, d_xr, d_ys, d_yr, d_send, d_recv)
    kv_out = remote(
        kv.at[:, pl.ds(tokens, half), :],
        kv.at[:, pl.ds(0, half), :],
        move_send.at[0],
        move_recv.at[0],
        place.along(1),
    )
    kv_back = remote(back_s, back_r, move_send.at[1], move_recv.at[1], place.along(-1))

    load.wait()
    low = mul(normed[...], down_ref[...])
    part = low.T
    pl.semaphore_wait(barrier, partners)
    ranks.start(part)
    tell(place, reach.at[0], 2)
    ranks.middle()
    pl.semaphore_wait(reach.at[0], 2)
    tell(place, reach.at[1], 4)
    low_t = ranks.end()
    low_bf = low_t.astype(BF16)
    low_rows = low_bf.astype(F32).T.astype(BF16)
    pl.semaphore_wait(reach.at[1], 2)
    tell(place, reach.at[2], 8)

    for i, base in enumerate((key_ref, value_ref)):
        lows = low_rows[:, depth * (i + 1) : depth * (i + 2)]
        kv[i, half:, :] = (base[...].astype(F32) + adapter_scale * mul(lows, pair_ref[i])).astype(
            BF16
        )
    kv_out.start()

    for copy in loads:
        copy.wait()
    query_low = low_rows[:, :depth]
    for h in range(heads):
        step = adapter_scale * mul(query_low, up_ref[:, h * HEAD_SIZE : (h + 1) * HEAD_SIZE])
        for p in range(2):
            rows = slice(h * half, (h + 1) * half)
            qs[p, rows, :] = (
                qs[p, rows, :].astype(F32) + step[p * half : (p + 1) * half]
            ).astype(BF16)

    low_q = low_bf[:depth].astype(F32)
    turned = pltpu.roll(low_q, half, 1)
    in_first = lax.broadcasted_iota(jnp.int32, low_q.shape, 1) < half
    zero = jnp.zeros_like(low_q)
    wide_low = (
        jnp.concatenate(
            [jnp.where(in_first, low_q, zero), jnp.where(in_first, zero, turned)], axis=0
        ).astype(BF16),
        jnp.concatenate(
            [jnp.where(in_first, turned, zero), jnp.where(in_first, zero, low_q)], axis=0
        ).astype(BF16),
    )

    stores = []

    def unit(first, count, p, pair):
        rows = slice(pair * tokens, (pair + 1) * tokens)
        keys = kv[0, first : first + count, :]
        values = kv[1, first : first + count, :]
        queries = qs[p, rows, :]
        grads = dos[p, rows, :]
        scores = mul(keys, queries, NT) * (SCALE * LOG2E)
        if count > half:
            scores = jnp.concatenate([scores[:half], scores[half:] + bias[...]], axis=0)
        else:
            scores = scores + bias[...]
        highest = jnp.max(scores, axis=0, keepdims=True)
        weights = jnp.exp2(scores - highest)
        probs = weights * (1.0 / jnp.sum(weights, axis=0, keepdims=True))
        probs_low = probs.astype(BF16)
        prob_grad = mul(values, grads, NT)
        row_dot = jnp.sum(probs * prob_grad, axis=0, keepdims=True)
        score_grad = (probs * (prob_grad - row_dot) * SCALE).astype(BF16)
        outs[p, rows, :] = mul(values, probs_low, TN).T.astype(BF16)
        query_grad = mul(keys, score_grad, TN).astype(BF16)
        dkv[0, first : first + count, :] += mul(score_grad, queries)
        dkv[1, first : first + count, :] += mul(probs_low, grads)
        one, two = 2 * pair, 2 * pair + 1
        ups = jnp.concatenate(
            [up_ref[:, h * HEAD_SIZE : (h + 1) * HEAD_SIZE] for h in (one, two)], axis=0
        )
        rank_acc[p] += mul(ups, query_grad)
        up_acc[pair] += mul(wide_low[p], query_grad, NT)
        for h in (one, two):
            copy = pltpu.make_async_copy(
                outs.at[p, pl.ds(h * half, half), :],
                attended_hbm.at[pl.ds(p * half, half), pl.ds(h * HEAD_SIZE, HEAD_SIZE)],
                store_sem.at[2 * h + p],
            )
            copy.start()
            stores.append(copy)

    unit(half, tokens, 1, 0)
    unit(half, tokens, 1, 1)
    unit(half, half, 0, 0)
    kv_out.wait()
    unit(0, tokens, 0, 2)
    unit(0, tokens, 0, 3)
    back_s[...] = dkv[:, :half, :].astype(BF16)
    kv_back.start()
    unit(half, half, 0, 1)
    unit(tokens, half, 1, 2)
    unit(tokens, half, 1, 3)

    first, second = rank_acc[0], rank_acc[1]
    ours = first[:depth] + pltpu.roll(first[depth:], half, 1)
    theirs = pltpu.roll(second[:depth], half, 1) + second[depth:]
    query_part = jnp.where(in_first, ours, theirs)
    kv_back.wait()
    dkv[:, tokens:, :] += back_r[...].astype(F32)
    parts, pair_grads = [query_part], []
    for i in range(2):
        grad = dkv[i, half:, :].astype(BF16)
        parts.append(mul(pair_ref[i], grad, NT))
        pair_grads.append(adapter_scale * mul(low_bf[depth * (i + 1) : depth * (i + 2)], grad))
    rank_grads.start(jnp.concatenate(parts, axis=0))
    zeros = jnp.zeros((8, 128), F32)
    for c in range(16):
        h, q = c // 2, c % 2
        top = 16 * (h % 2) + 8 * q
        upper = adapter_scale * up_acc[h // 2, top : top + 8, :]
        lower = pair_grads[c // 2][8 * q : 8 * q + 8] if c < 4 else zeros
        e_mine[c] = jnp.concatenate([upper, lower], axis=0).astype(BF16)
    early.start()
    rank_grads.middle()
    pl.semaphore_wait(reach.at[2], 2)
    early.middle()
    rank_grad = (adapter_scale * rank_grads.end()).astype(BF16)
    for j in range(8):
        columns = slice(128 * j, 128 * j + 128)
        down = mul(rank_grad, normed[:, columns])
        g_mine[2 * j] = down[:24].astype(BF16)
        g_mine[2 * j + 1] = down[24:].astype(BF16)
    late.start()
    late.middle()
    early.late()
    early.end()
    for c in range(16):
        value = e_full[c].astype(F32)
        up_out[8 * (c % 2) : 8 * (c % 2) + 8, 128 * (c // 2) : 128 * (c // 2) + 128] = value[:8]
        if c < 4:
            pair_out[8 * c : 8 * c + 8, :] = value[8:]
    late.late()
    late.end()
    for c in range(16):
        down_out[24 * (c % 2) : 24 * (c % 2) + 24, 128 * (c // 2) : 128 * (c // 2) + 128] = g_full[
            c
        ].astype(F32)
    for copy in stores:
        copy.wait()
    early.drain()
    late.drain()


def token_sum_scratch(rows):
    return [
        pltpu.VMEM((16, rows, 128), BF16),
        pltpu.VMEM((16, rows, 128), BF16),
        pltpu.VMEM((8, rows, 128), BF16),
        pltpu.VMEM((16, rows, 128), BF16),
        pltpu.SemaphoreType.DMA((40,)),
        pltpu.SemaphoreType.DMA((40,)),
    ]


def tensor_sum_scratch(ranks, tokens):
    return [
        pltpu.VMEM((ranks, tokens), BF16),
        pltpu.VMEM((ranks, tokens), BF16),
        pltpu.VMEM((ranks, tokens), BF16),
        pltpu.VMEM((3, ranks, tokens), BF16),
        pltpu.SemaphoreType.DMA((4,)),
        pltpu.SemaphoreType.DMA((4,)),
    ]


def on_device(normed, query_base, key_base, value_base, down, up, pair, grad):
    vmem = pl.BlockSpec(memory_space=pltpu.VMEM)
    hbm = pl.BlockSpec(memory_space=pl.ANY)
    tokens, width = normed.shape[1:]
    depth = up.shape[0]
    ranks = down.shape[1]
    heads = width // HEAD_SIZE
    half = tokens // 2
    stacked = (2, heads * half, HEAD_SIZE)
    attended, down_grad, up_grad, pair_grad = pl.pallas_call(
        kernel,
        out_shape=(
            jax.ShapeDtypeStruct((tokens, width), BF16),
            jax.ShapeDtypeStruct((ranks, width), F32),
            jax.ShapeDtypeStruct((depth, width), F32),
            jax.ShapeDtypeStruct((2 * depth, HEAD_SIZE), F32),
        ),
        in_specs=[hbm, hbm, vmem, vmem, vmem, vmem, vmem, hbm],
        out_specs=(hbm, vmem, vmem, vmem),
        scratch_shapes=[
            pltpu.VMEM((tokens, width), BF16),
            pltpu.VMEM(stacked, BF16),
            pltpu.VMEM(stacked, BF16),
            pltpu.VMEM(stacked, BF16),
            pltpu.VMEM((2, tokens + half, HEAD_SIZE), BF16),
            pltpu.VMEM((2, tokens + half, HEAD_SIZE), F32),
            pltpu.VMEM((half, tokens), F32),
            pltpu.VMEM((2, 2 * depth, tokens), F32),
            pltpu.VMEM((heads // 2, 2 * depth, HEAD_SIZE), F32),
            pltpu.VMEM((2, half, HEAD_SIZE), BF16),
            pltpu.VMEM((2, half, HEAD_SIZE), BF16),
            pltpu.SemaphoreType.DMA((1 + 4 * heads,)),
            pltpu.SemaphoreType.DMA((2 * heads,)),
            pltpu.SemaphoreType.DMA((2,)),
            pltpu.SemaphoreType.DMA((2,)),
            pltpu.SemaphoreType.REGULAR((3,)),
        ]
        + tensor_sum_scratch(ranks, tokens)
        + tensor_sum_scratch(ranks, tokens)
        + token_sum_scratch(16)
        + token_sum_scratch(24),
        compiler_params=pltpu.CompilerParams(
            collective_id=0, has_side_effects=True, vmem_limit_bytes=56 * 1024 * 1024
        ),
    )(normed[0], query_base[0], key_base[0], value_base[0], down, up, pair, grad[0])
    return (attended[None], down_grad.T, up_grad, pair_grad.reshape(2, depth, -1))


def solution(mesh):
    split = Mesh(
        mesh.devices.reshape(2, 2, mesh.shape["context"], 2, 4),
        ("dp_0", "dp_1", "context", "tensor_0", "tensor_1"),
    )
    placed = (
        P(DP, "context", TENSOR),
        P(DP, "context", TENSOR),
        P(DP, "context", TENSOR),
        P(DP, "context", TENSOR),
        P(TENSOR, None),
        P(None, TENSOR),
        P(None, None, TENSOR),
        P(DP, "context", TENSOR),
    )
    return jax.shard_map(
        on_device,
        mesh=split,
        in_specs=placed,
        out_specs=(
            P(DP, "context", TENSOR),
            P(TENSOR, None),
            P(None, TENSOR),
            P(None, None, TENSOR),
        ),
        check_vma=False,
    )
```

time: 161 us -> 79.5 us (0.49)
  starting transfers between devices: 32.9 us -> 0 us
  matrix products: 26.7 us -> 0 us
  Pallas kernels: 50.2 us -> 72.5 us
  blocking collectives: 13.9 us -> 0 us
  other arithmetic: 12 us -> 0 us
  local copies, waits for them, and re-layouts: 17 us -> 6.02 us
  waiting for transfers between devices: 5.43 us -> 0 us
    dot_general x58 -> x0, matrix products: 26.7 us -> none  [the longest x8 7.73 us: attend_single(): jnp.einsum('gtu,tgd->ugd', probs_low, grads, preferred_element_type=jnp.f...]
    ppermute x4 -> x0, starting transfers between devices: 25.4 us -> none  [shifted(): return lax.ppermute(value, axis, pairs)]
    pallas_call x1, Pallas kernels: 50.2 us -> 72.5 us  [on_device(): pl.pallas_call(kernel, out_shape=(jax.ShapeDtypeStruct((tokens, width), B...]
    all_gather x2 -> x0, blocking collectives: 13.9 us -> none  [gather_in_order(): tiles = lax.all_gather(tiles, axes[k])]
    all_to_all x1 -> x0, starting transfers between devices: 7.47 us -> none  [sent_and_summed(): tiles = lax.all_to_all(cut_along(shard, dim, count), axis, 0, 0, tiled=True)]
    reduce_sum x13 -> x0, other arithmetic: 6.5 us -> none  [the longest x2 3.33 us: attend(): value_gradient = jnp.sum(results[3], axis=0)]
    all_to_all x1 -> x0, waiting for transfers between devices: 5.3 us -> none  [sent_and_summed(): tiles = lax.all_to_all(cut_along(shard, dim, count), axis, 0, 0, tiled=True)]
    while x24 -> x0, local copies, waits for them, and re-layouts: 3.97 us -> none
  transfers between devices with their start and end apart: 5 -> 0, of which waited for: 2 -> 0; matrix products, arithmetic and copies ran while one was open for 14% -> 0% of each run, Pallas kernels for 0% -> 0%
where the time goes in v2:
time: 79.5 us; the launch traced here: 79.1 us
  Pallas kernels  72.5 us (91%)
  local copies, waits for them, and re-layouts  6.02 us (8%)
    pallas_call x1, Pallas kernels, on_device(): pl.pallas_call(kernel, out_shape=(jax.ShapeDtypeStruct((tokens, width), B...  72.5 us
    unnamed x11, local copies, waits for them, and re-layouts  6.02 us

profile of v2, /device:TPU:1, one launch (start us, length us, event | category | flops | bytes accessed | tf_op | source)
XLA Modules:
  0.0 79.1 jit_solution(10520131337437565055)
XLA Ops:
  0.6 1.7 %copy.12.down_ref = bf16[1024,48]{1,0:T(8,128)(2,1)} copy(bf16[1024,48]{0,1:T(8,128)(2,1)} %param.12) | data formatting | bytes 196608 | tf_op args[4]
  2.4 72.5 %shard_map.111 = (bf16[384,1024]{1,0:T(8,128)(2,1)}, f32[48,1024]{1,0:T(8,128)}, f32[16,1024]{1,0:T(8,128)}, f32[32,128]{1,0:T(8,128)}) custom-call(bf16[384,1024]{1,0:T(8,128)(2,1)} %bitcast.9, bf16[384,1024]{1,0:T(8,128)(2,1)} %bitcast.10, bf16[384,128]{1,0:T(8,128)(2,1)} %bitcast.13, bf16[384,128]{1,0:T(8,128)(2,1)} %bitcast.14, ...), custom_call_target="tpu_custom_call" | custom-call | tf_op jit(solution)/shard_map/pallas_call | solution.py:485
  74.8 0.0 copy-start
  74.8 2.1 %copy.17 = bf16[1,384,1024]{2,1,0:T(8,128)(2,1)} copy(bf16[1,384,1024]{2,1,0:T(8,128)(2,1)} %bitcast.8) | data formatting | bytes 1572864
  76.9 0.0 copy-done
  76.9 0.0 copy-start.1
  76.9 0.7 copy.18
  77.6 0.2 copy-done.1
  77.8 0.0 copy-start.2
  77.8 0.6 copy.19
  78.4 0.1 copy-done.2
  78.5 0.6 copy.20
Async XLA Ops:
  74.8 2.1 %copy-start = (f32[48,1024]{1,0:T(8,128)S(1)}, f32[48,1024]{1,0:T(8,128)}, u32[]{:S(2)}) copy-start(f32[48,1024]{1,0:T(8,128)} %get-tuple-element.9) | copy-start | bytes 589828
  76.9 0.9 %copy-start.1 = (f32[16,1024]{1,0:T(8,128)S(1)}, f32[16,1024]{1,0:T(8,128)}, u32[]{:S(2)}) copy-start(f32[16,1024]{1,0:T(8,128)} %get-tuple-element.18) | copy-start | bytes 196612
  77.8 0.7 copy-start.2

commit v3 on v2

--- a/solution.py
+++ b/solution.py
@@ -69,36 +69,46 @@
     def __init__(self, place, xs, xr, ys, yr, send, recv):
         self.xs, self.xr, self.ys, self.yr = xs, xr, ys, yr
         half = lax.rem(place.half + 1, 2)
-        self.first = remote(xs, xr, send.at[0], recv.at[0], {"tensor_0": half})
+        chunks = range(xs.shape[0])
+        self.first = [
+            remote(
+                xs.at[c], xr.at[c], send.at[4 * c], recv.at[4 * c], {"tensor_0": half}
+            )
+            for c in chunks
+        ]
         self.second = [
-            remote(
-                ys,
-                yr.at[k - 1],
-                send.at[k],
-                recv.at[k],
-                {"tensor_1": lax.rem(place.y + k, 4)},
-            )
-            for k in (2, 1, 3)
+            [
+                remote(
+                    ys.at[c],
+                    yr.at[c, k - 1],
+                    send.at[4 * c + k],
+                    recv.at[4 * c + k],
+                    {"tensor_1": lax.rem(place.y + k, 4)},
+                )
+                for k in (2, 1, 3)
+            ]
+            for c in chunks
         ]
-
-    def start(self, part):
-        self.part = part
-        self.xs[...] = part.astype(BF16)
-        self.first.start()
-
-    def middle(self):
-        self.first.wait()
-        self.total = self.part + self.xr[...].astype(F32)
-        self.ys[...] = self.total.astype(BF16)
-        for copy in self.second:
+        self.part, self.total = {}, {}
+
+    def start(self, c, part):
+        self.part[c] = part
+        self.xs[c] = part.astype(BF16)
+        self.first[c].start()
+
+    def middle(self, c):
+        self.first[c].wait()
+        self.total[c] = self.part[c] + self.xr[c].astype(F32)
+        self.ys[c] = self.total[c].astype(BF16)
+        for copy in self.second[c]:
             copy.start()
 
-    def end(self):
-        for copy in self.second:
+    def end(self, c):
+        for copy in self.second[c]:
             copy.wait()
-        total = self.total
+        total = self.total[c]
         for k in range(3):
-            total = total + self.yr[k].astype(F32)
+            total = total + self.yr[c, k].astype(F32)
         return total
 
 
@@ -211,29 +221,34 @@
 def kernel(
     normed_hbm,
     query_hbm,
-    key_ref,
-    value_ref,
-    down_ref,
-    up_ref,
-    pair_ref,
+    key_hbm,
+    value_hbm,
+    down_hbm,
+    up_hbm,
+    pair_hbm,
     grad_hbm,
-    attended_hbm,
+    outs,
     down_out,
     up_out,
     pair_out,
     normed,
     qs,
     dos,
-    outs,
+    base,
+    down_ref,
+    up_ref,
+    pair_ref,
     kv,
     dkv,
     bias,
     rank_acc,
     up_acc,
+    low_s,
+    low_r,
+    base_r,
     back_s,
     back_r,
     load_sem,
-    store_sem,
     move_send,
     move_recv,
     reach,
@@ -263,25 +278,72 @@
     grecv,
 ):
     place = Place()
-    tokens = normed.shape[0]
+    tokens, width = normed.shape
     half = tokens // 2
     depth = up_ref.shape[0]
     heads = up_ref.shape[1] // HEAD_SIZE
-
-    load = pltpu.make_async_copy(normed_hbm, normed, load_sem.at[0])
-    load.start()
+    tail = low_r.shape[2]
+    pad = tail - half
+
+    index = 0
+
+    def fetch(source, target):
+        nonlocal index
+        copy = pltpu.make_async_copy(source, target, load_sem.at[index])
+        copy.start()
+        index += 1
+        return copy
+
+    down_load = fetch(down_hbm, down_ref)
+    halves = [pl.ds(k * (width // 2), width // 2) for k in range(2)]
+    normed_loads = [fetch(normed_hbm.at[:, k], normed.at[:, k]) for k in halves]
+    base_loads = [fetch(key_hbm, base.at[0]), fetch(value_hbm, base.at[1])]
+    weight_loads = [fetch(pair_hbm, pair_ref), fetch(up_hbm, up_ref)]
     loads = []
-    for source, target, first in ((query_hbm, qs, 1), (grad_hbm, dos, 1 + 2 * heads)):
+    for source, target in ((query_hbm, qs), (grad_hbm, dos)):
         for h in range(heads):
-            for part in range(2):
-                copy = pltpu.make_async_copy(
-                    source.at[pl.ds(part * half, half), pl.ds(h * HEAD_SIZE, HEAD_SIZE)],
-                    target.at[part, pl.ds(h * half, half), :],
-                    load_sem.at[first + 2 * h + part],
+            for p in range(2):
+                loads.append(
+                    fetch(
+                        source.at[pl.ds(p * half, half), pl.ds(h * HEAD_SIZE, HEAD_SIZE)],
+                        target.at[p, pl.ds(h * half, half), :],
+                    )
                 )
-                copy.start()
-                loads.append(copy)
     barrier, partners = greet(place)
+
+    early = TokenSum(place, e_mine, e_got, e_spread, e_full, esend, erecv)
+    late = TokenSum(place, g_mine, g_got, g_spread, g_full, gsend, grecv)
+    ranks = TensorSum(place, a_xs, a_xr, a_ys, a_yr, a_send, a_recv)
+    rank_grads = TensorSum(place, d_xs, d_xr, d_ys, d_yr, d_send, d_recv)
+    base_out = remote(
+        base.at[:, pl.ds(half, half), :], base_r, move_send.at[0], move_recv.at[0], place.along(1)
+    )
+    low_out = [
+        remote(
+            low_s.at[i, :, pl.ds(tokens - tail, tail)],
+            low_r.at[i],
+            move_send.at[1 + i],
+            move_recv.at[1 + i],
+            place.along(1),
+        )
+        for i in range(2)
+    ]
+    back = remote(back_s, back_r, move_send.at[3], move_recv.at[3], place.along(-1))
+
+    down_load.wait()
+    low = None
+    for k, copy in enumerate(normed_loads):
+        copy.wait()
+        columns = slice(k * (width // 2), (k + 1) * (width // 2))
+        term = mul(down_ref[:, columns], normed[:, columns], NT)
+        low = term if low is None else low + term
+    pl.semaphore_wait(barrier, partners)
+    for c in (1, 2, 0):
+        ranks.start(c, low[depth * c : depth * (c + 1)])
+    for copy in base_loads:
+        copy.wait()
+    base_out.start()
+    tell(place, reach.at[0], 2)
 
     key_ids = lax.broadcasted_iota(jnp.int32, (half, tokens), 0)
     lanes = lax.broadcasted_iota(jnp.int32, (half, tokens), 1)
@@ -291,44 +353,23 @@
     rank_acc[...] = jnp.zeros_like(rank_acc)
     up_acc[...] = jnp.zeros_like(up_acc)
 
-    early = TokenSum(place, e_mine, e_got, e_spread, e_full, esend, erecv)
-    late = TokenSum(place, g_mine, g_got, g_spread, g_full, gsend, grecv)
-    ranks = TensorSum(place, a_xs, a_xr, a_ys, a_yr, a_send, a_recv)
-    rank_grads = TensorSum(place, d_xs, d_xr, d_ys, d_yr, d_send, d_recv)
-    kv_out = remote(
-        kv.at[:, pl.ds(tokens, half), :],
-        kv.at[:, pl.ds(0, half), :],
-        move_send.at[0],
-        move_recv.at[0],
-        place.along(1),
-    )
-    kv_back = remote(back_s, back_r, move_send.at[1], move_recv.at[1], place.along(-1))
-
-    load.wait()
-    low = mul(normed[...], down_ref[...])
-    part = low.T
-    pl.semaphore_wait(barrier, partners)
-    ranks.start(part)
-    tell(place, reach.at[0], 2)
-    ranks.middle()
+    for c in (1, 2, 0):
+        ranks.middle(c)
     pl.semaphore_wait(reach.at[0], 2)
     tell(place, reach.at[1], 4)
-    low_t = ranks.end()
-    low_bf = low_t.astype(BF16)
-    low_rows = low_bf.astype(F32).T.astype(BF16)
-    pl.semaphore_wait(reach.at[1], 2)
-    tell(place, reach.at[2], 8)
-
-    for i, base in enumerate((key_ref, value_ref)):
-        lows = low_rows[:, depth * (i + 1) : depth * (i + 2)]
-        kv[i, half:, :] = (base[...].astype(F32) + adapter_scale * mul(lows, pair_ref[i])).astype(
-            BF16
-        )
-    kv_out.start()
-
+    for copy in weight_loads:
+        copy.wait()
+    for i in range(2):
+        low_s[i] = ranks.end(1 + i).astype(BF16)
+        low_out[i].start()
+        kv[i, half:, :] = (
+            base[i].astype(F32) + adapter_scale * mul(low_s[i], pair_ref[i], TN)
+        ).astype(BF16)
+    low_q = ranks.end(0).astype(BF16)
+    low_q32 = low_q.astype(F32)
+    query_low = low_q32.T.astype(BF16)
     for copy in loads:
         copy.wait()
-    query_low = low_rows[:, :depth]
     for h in range(heads):
         step = adapter_scale * mul(query_low, up_ref[:, h * HEAD_SIZE : (h + 1) * HEAD_SIZE])
         for p in range(2):
@@ -337,20 +378,17 @@
                 qs[p, rows, :].astype(F32) + step[p * half : (p + 1) * half]
             ).astype(BF16)
 
-    low_q = low_bf[:depth].astype(F32)
-    turned = pltpu.roll(low_q, half, 1)
+    turned = pltpu.roll(low_q32, half, 1)
     in_first = lax.broadcasted_iota(jnp.int32, low_q.shape, 1) < half
-    zero = jnp.zeros_like(low_q)
+    zero = jnp.zeros_like(low_q32)
     wide_low = (
         jnp.concatenate(
-            [jnp.where(in_first, low_q, zero), jnp.where(in_first, zero, turned)], axis=0
+            [jnp.where(in_first, low_q32, zero), jnp.where(in_first, zero, turned)], axis=0
         ).astype(BF16),
         jnp.concatenate(
-            [jnp.where(in_first, turned, zero), jnp.where(in_first, zero, low_q)], axis=0
+            [jnp.where(in_first, turned, zero), jnp.where(in_first, zero, low_q32)], axis=0
         ).astype(BF16),
     )
-
-    stores = []
 
     def unit(first, count, p, pair):
         rows = slice(pair * tokens, (pair + 1) * tokens)
@@ -372,31 +410,29 @@
         score_grad = (probs * (prob_grad - row_dot) * SCALE).astype(BF16)
         outs[p, rows, :] = mul(values, probs_low, TN).T.astype(BF16)
         query_grad = mul(keys, score_grad, TN).astype(BF16)
-        dkv[0, first : first + count, :] += mul(score_grad, queries)
-        dkv[1, first : first + count, :] += mul(probs_low, grads)
+        dkv[0, pad + first : pad + first + count, :] += mul(score_grad, queries)
+        dkv[1, pad + first : pad + first + count, :] += mul(probs_low, grads)
         one, two = 2 * pair, 2 * pair + 1
         ups = jnp.concatenate(
             [up_ref[:, h * HEAD_SIZE : (h + 1) * HEAD_SIZE] for h in (one, two)], axis=0
         )
         rank_acc[p] += mul(ups, query_grad)
         up_acc[pair] += mul(wide_low[p], query_grad, NT)
-        for h in (one, two):
-            copy = pltpu.make_async_copy(
-                outs.at[p, pl.ds(h * half, half), :],
-                attended_hbm.at[pl.ds(p * half, half), pl.ds(h * HEAD_SIZE, HEAD_SIZE)],
-                store_sem.at[2 * h + p],
-            )
-            copy.start()
-            stores.append(copy)
 
     unit(half, tokens, 1, 0)
     unit(half, tokens, 1, 1)
-    unit(half, half, 0, 0)
-    kv_out.wait()
+    base_out.wait()
+    for i in range(2):
+        low_out[i].wait()
+        step = adapter_scale * mul(low_r[i], pair_ref[i], TN)
+        kv[i, :half, :] = (base_r[i].astype(F32) + step[pad:]).astype(BF16)
     unit(0, tokens, 0, 2)
     unit(0, tokens, 0, 3)
-    back_s[...] = dkv[:, :half, :].astype(BF16)
-    kv_back.start()
+    far_grads = [dkv[i, :tail, :].astype(BF16) for i in range(2)]
+    for i in range(2):
+        back_s[i] = mul(pair_ref[i], far_grads[i], NT).astype(BF16)
+    back.start()
+    unit(half, half, 0, 0)
     unit(half, half, 0, 1)
     unit(tokens, half, 1, 2)
     unit(tokens, half, 1, 3)
@@ -404,15 +440,17 @@
     first, second = rank_acc[0], rank_acc[1]
     ours = first[:depth] + pltpu.roll(first[depth:], half, 1)
     theirs = pltpu.roll(second[:depth], half, 1) + second[depth:]
-    query_part = jnp.where(in_first, ours, theirs)
-    kv_back.wait()
-    dkv[:, tokens:, :] += back_r[...].astype(F32)
-    parts, pair_grads = [query_part], []
+    rank_grads.start(0, jnp.where(in_first, ours, theirs))
+    grads = [dkv[i, tail:, :].astype(BF16) for i in range(2)]
+    parts = [mul(pair_ref[i], grads[i], NT) for i in range(2)]
+    back.wait()
     for i in range(2):
-        grad = dkv[i, half:, :].astype(BF16)
-        parts.append(mul(pair_ref[i], grad, NT))
-        pair_grads.append(adapter_scale * mul(low_bf[depth * (i + 1) : depth * (i + 2)], grad))
-    rank_grads.start(jnp.concatenate(parts, axis=0))
+        near = parts[i][:, : tokens - tail]
+        far = parts[i][:, tokens - tail :] + back_r[i].astype(F32)
+        rank_grads.start(1 + i, jnp.concatenate([near, far], axis=1))
+    pair_grads = [
+        adapter_scale * (mul(low_s[i], grads[i]) + mul(low_r[i], far_grads[i])) for i in range(2)
+    ]
     zeros = jnp.zeros((8, 128), F32)
     for c in range(16):
         h, q = c // 2, c % 2
@@ -420,17 +458,22 @@
         upper = adapter_scale * up_acc[h // 2, top : top + 8, :]
         lower = pair_grads[c // 2][8 * q : 8 * q + 8] if c < 4 else zeros
         e_mine[c] = jnp.concatenate([upper, lower], axis=0).astype(BF16)
+    for c in range(3):
+        rank_grads.middle(c)
     early.start()
-    rank_grads.middle()
-    pl.semaphore_wait(reach.at[2], 2)
-    early.middle()
-    rank_grad = (adapter_scale * rank_grads.end()).astype(BF16)
+    pl.semaphore_wait(reach.at[1], 2)
+    tell(place, reach.at[2], 8)
+    rank_grad = jnp.concatenate(
+        [(adapter_scale * rank_grads.end(c)).astype(BF16) for c in range(3)], axis=0
+    )
     for j in range(8):
         columns = slice(128 * j, 128 * j + 128)
         down = mul(rank_grad, normed[:, columns])
         g_mine[2 * j] = down[:24].astype(BF16)
         g_mine[2 * j + 1] = down[24:].astype(BF16)
     late.start()
+    pl.semaphore_wait(reach.at[2], 2)
+    early.middle()
     late.middle()
     early.late()
     early.end()
@@ -445,10 +488,28 @@
         down_out[24 * (c % 2) : 24 * (c % 2) + 24, 128 * (c // 2) : 128 * (c // 2) + 128] = g_full[
             c
         ].astype(F32)
-    for copy in stores:
-        copy.wait()
     early.drain()
     late.drain()
+
+
+def store_kernel(outs, down, up, pair, attended_hbm, down_hbm, up_hbm, pair_hbm, sem):
+    half = attended_hbm.shape[0] // 2
+    heads = attended_hbm.shape[1] // HEAD_SIZE
+    copies = [
+        pltpu.make_async_copy(
+            outs.at[p, pl.ds(h * half, half), :],
+            attended_hbm.at[pl.ds(p * half, half), pl.ds(h * HEAD_SIZE, HEAD_SIZE)],
+            sem.at[2 * h + p],
+        )
+        for h in range(heads)
+        for p in range(2)
+    ]
+    for k, (source, target) in enumerate(((down, down_hbm), (up, up_hbm), (pair, pair_hbm))):
+        copies.append(pltpu.make_async_copy(source, target, sem.at[2 * heads + k]))
+    for copy in copies:
+        copy.start()
+    for copy in copies:
+        copy.wait()
 
 
 def token_sum_scratch(rows):
@@ -462,62 +523,81 @@
     ]
 
 
-def tensor_sum_scratch(ranks, tokens):
+def tensor_sum_scratch(chunks, rows, tokens):
     return [
-        pltpu.VMEM((ranks, tokens), BF16),
-        pltpu.VMEM((ranks, tokens), BF16),
-        pltpu.VMEM((ranks, tokens), BF16),
-        pltpu.VMEM((3, ranks, tokens), BF16),
-        pltpu.SemaphoreType.DMA((4,)),
-        pltpu.SemaphoreType.DMA((4,)),
+        pltpu.VMEM((chunks, rows, tokens), BF16),
+        pltpu.VMEM((chunks, rows, tokens), BF16),
+        pltpu.VMEM((chunks, rows, tokens), BF16),
+        pltpu.VMEM((chunks, 3, rows, tokens), BF16),
+        pltpu.SemaphoreType.DMA((4 * chunks,)),
+        pltpu.SemaphoreType.DMA((4 * chunks,)),
     ]
 
 
 def on_device(normed, query_base, key_base, value_base, down, up, pair, grad):
     vmem = pl.BlockSpec(memory_space=pltpu.VMEM)
-    hbm = pl.BlockSpec(memory_space=pl.ANY)
+    hbm = pl.BlockSpec(memory_space=pltpu.HBM)
     tokens, width = normed.shape[1:]
     depth = up.shape[0]
     ranks = down.shape[1]
     heads = width // HEAD_SIZE
     half = tokens // 2
+    tail = 256
     stacked = (2, heads * half, HEAD_SIZE)
+    results = pl.pallas_call(
+        kernel,
+        out_shape=(
+            pltpu.VMEM(stacked, BF16),
+            pltpu.VMEM((ranks, width), F32),
+            pltpu.VMEM((depth, width), F32),
+            pltpu.VMEM((2 * depth, HEAD_SIZE), F32),
+        ),
+        in_specs=[hbm] * 8,
+        out_specs=(vmem,) * 4,
+        scratch_shapes=[
+            pltpu.VMEM((tokens, width), BF16),
+            pltpu.VMEM(stacked, BF16),
+            pltpu.VMEM(stacked, BF16),
+            pltpu.VMEM((2, tokens, HEAD_SIZE), BF16),
+            pltpu.VMEM((ranks, width), BF16),
+            pltpu.VMEM((depth, width), BF16),
+            pltpu.VMEM((2, depth, HEAD_SIZE), BF16),
+            pltpu.VMEM((2, tokens + half, HEAD_SIZE), BF16),
+            pltpu.VMEM((2, tokens + tail, HEAD_SIZE), F32),
+            pltpu.VMEM((half, tokens), F32),
+            pltpu.VMEM((2, 2 * depth, tokens), F32),
+            pltpu.VMEM((heads // 2, 2 * depth, HEAD_SIZE), F32),
+            pltpu.VMEM((2, depth, tokens), BF16),
+            pltpu.VMEM((2, depth, tail), BF16),
+            pltpu.VMEM((2, half, HEAD_SIZE), BF16),
+            pltpu.VMEM((2, depth, tail), BF16),
+            pltpu.VMEM((2, depth, tail), BF16),
+            pltpu.SemaphoreType.DMA((7 + 4 * heads,)),
+            pltpu.SemaphoreType.DMA((4,)),
+            pltpu.SemaphoreType.DMA((4,)),
+            pltpu.SemaphoreType.REGULAR((3,)),
+        ]
+        + tensor_sum_scratch(3, depth, tokens)
+        + tensor_sum_scratch(3, depth, tokens)
+        + token_sum_scratch(16)
+        + token_sum_scratch(24),
+        compiler_params=pltpu.CompilerParams(
+            collective_id=0, has_side_effects=True, vmem_limit_bytes=60 * 1024 * 1024
+        ),
+    )(normed[0], query_base[0], key_base[0], value_base[0], down.T, up, pair, grad[0])
     attended, down_grad, up_grad, pair_grad = pl.pallas_call(
-        kernel,
+        store_kernel,
         out_shape=(
             jax.ShapeDtypeStruct((tokens, width), BF16),
             jax.ShapeDtypeStruct((ranks, width), F32),
             jax.ShapeDtypeStruct((depth, width), F32),
             jax.ShapeDtypeStruct((2 * depth, HEAD_SIZE), F32),
         ),
-        in_specs=[hbm, hbm, vmem, vmem, vmem, vmem, vmem, hbm],
-        out_specs=(hbm, vmem, vmem, vmem),
-        scratch_shapes=[
-            pltpu.VMEM((tokens, width), BF16),
-            pltpu.VMEM(stacked, BF16),
-            pltpu.VMEM(stacked, BF16),
-            pltpu.VMEM(stacked, BF16),
-            pltpu.VMEM((2, tokens + half, HEAD_SIZE), BF16),
-            pltpu.VMEM((2, tokens + half, HEAD_SIZE), F32),
-            pltpu.VMEM((half, tokens), F32),
-            pltpu.VMEM((2, 2 * depth, tokens), F32),
-            pltpu.VMEM((heads // 2, 2 * depth, HEAD_SIZE), F32),
-            pltpu.VMEM((2, half, HEAD_SIZE), BF16),
-            pltpu.VMEM((2, half, HEAD_SIZE), BF16),
-            pltpu.SemaphoreType.DMA((1 + 4 * heads,)),
-            pltpu.SemaphoreType.DMA((2 * heads,)),
-            pltpu.SemaphoreType.DMA((2,)),
-            pltpu.SemaphoreType.DMA((2,)),
-            pltpu.SemaphoreType.REGULAR((3,)),
-        ]
-        + tensor_sum_scratch(ranks, tokens)
-        + tensor_sum_scratch(ranks, tokens)
-        + token_sum_scratch(16)
-        + token_sum_scratch(24),
-        compiler_params=pltpu.CompilerParams(
-            collective_id=0, has_side_effects=True, vmem_limit_bytes=56 * 1024 * 1024
-        ),
-    )(normed[0], query_base[0], key_base[0], value_base[0], down, up, pair, grad[0])
+        in_specs=[vmem] * 4,
+        out_specs=(hbm,) * 4,
+        scratch_shapes=[pltpu.SemaphoreType.DMA((2 * heads + 3,))],
+        compiler_params=pltpu.CompilerParams(vmem_limit_bytes=1024 * 1024),
+    )(*results)
     return (attended[None], down_grad.T, up_grad, pair_grad.reshape(2, depth, -1))
 
 

time: 79.5 us -> 71.1 us (0.89)
  local copies, waits for them, and re-layouts: 6.02 us -> 0 us
  Pallas kernels: 72.5 us -> 70.3 us
    unnamed x11 -> x0, local copies, waits for them, and re-layouts: 6.02 us -> none
    pallas_call x1 -> x2, Pallas kernels: 72.5 us -> 70.3 us  [the longest x1 69.2 us: on_device(): pl.pallas_call(kernel, out_shape=(pltpu.VMEM(stacked, BF16), pltpu.VMEM((...]
where the time goes in v3:
time: 71.1 us; the launch traced here: 70.9 us
  Pallas kernels  70.3 us (99%)
    pallas_call x1, Pallas kernels, on_device(): pl.pallas_call(kernel, out_shape=(pltpu.VMEM(stacked, BF16), pltpu.VMEM((...  69.2 us

profile of v3, /device:TPU:1, one launch (start us, length us, event | category | flops | bytes accessed | tf_op | source)
XLA Modules:
  0.0 70.9 jit_solution(4977647699974663046)
XLA Ops:
  0.6 69.2 %shard_map.111 = (bf16[2,1536,128]{2,1,0:T(8,128)(2,1)S(1)}, f32[48,1024]{1,0:T(8,128)S(1)}, f32[16,1024]{1,0:T(8,128)S(1)}, f32[32,128]{1,0:T(8,128)S(1)}) custom-call(bf16[384,1024]{1,0:T(8,128)(2,1)} %bitcast.9, bf16[384,1024]{1,0:T(8,128)(2,1)} %bitcast.10, bf16[384,128]{1,0:T(8,128)(2,1)} %bitcast.12, bf16[384,128]{1,0:T(8,128)(2,1)} %bitcast.13, ...), custom_call_target="tpu_custom_call" | custom-call | tf_op jit(solution)/shard_map/pallas_call | solution.py:547
  69.8 1.1 %shard_map.112 = (bf16[384,1024]{1,0:T(8,128)(2,1)}, f32[48,1024]{1,0:T(8,128)}, f32[16,1024]{1,0:T(8,128)}, f32[32,128]{1,0:T(8,128)}) custom-call(bf16[2,1536,128]{2,1,0:T(8,128)(2,1)S(1)} %get-tuple-element.12.outs, f32[48,1024]{1,0:T(8,128)S(1)} %get-tuple-element.13.down, f32[16,1024]{1,0:T(8,128)S(1)} %get-tuple-element.14.up, ...), custom_call_target="tpu_custom_call" | custom-call | tf_op jit(solution)/shard_map/pallas_call | solution.py:588

commit v4 on v3

--- a/solution.py
+++ b/solution.py
@@ -18,6 +18,7 @@
 BF16 = jnp.bfloat16
 STEPS = (2, 1, -1, 0)
 FAR = (4, 3, 5, 2, 6, 1, 7)
+STORES = 4
 
 
 class Place:
@@ -47,11 +48,11 @@
 
 
 def near_partners():
-    for step in STEPS:
+    for i, step in enumerate(STEPS):
         for a in (1, 0):
             for b in (1, 0):
                 if a or b or step:
-                    yield a, b, step, (a * 2 + b) * 4 + STEPS.index(step)
+                    yield a, b, (-step if step == 2 and b else step), (a * 2 + b) * 4 + i
 
 
 def remote(src, dst, send_sem, recv_sem, device):
@@ -276,6 +277,12 @@
     g_full,
     gsend,
     grecv,
+    h_mine,
+    h_got,
+    h_spread,
+    h_full,
+    hsend,
+    hrecv,
 ):
     place = Place()
     tokens, width = normed.shape
@@ -297,22 +304,13 @@
     down_load = fetch(down_hbm, down_ref)
     halves = [pl.ds(k * (width // 2), width // 2) for k in range(2)]
     normed_loads = [fetch(normed_hbm.at[:, k], normed.at[:, k]) for k in halves]
+    barrier, partners = greet(place)
     base_loads = [fetch(key_hbm, base.at[0]), fetch(value_hbm, base.at[1])]
     weight_loads = [fetch(pair_hbm, pair_ref), fetch(up_hbm, up_ref)]
-    loads = []
-    for source, target in ((query_hbm, qs), (grad_hbm, dos)):
-        for h in range(heads):
-            for p in range(2):
-                loads.append(
-                    fetch(
-                        source.at[pl.ds(p * half, half), pl.ds(h * HEAD_SIZE, HEAD_SIZE)],
-                        target.at[p, pl.ds(h * half, half), :],
-                    )
-                )
-    barrier, partners = greet(place)
 
     early = TokenSum(place, e_mine, e_got, e_spread, e_full, esend, erecv)
     late = TokenSum(place, g_mine, g_got, g_spread, g_full, gsend, grecv)
+    last = TokenSum(place, h_mine, h_got, h_spread, h_full, hsend, hrecv)
     ranks = TensorSum(place, a_xs, a_xr, a_ys, a_yr, a_send, a_recv)
     rank_grads = TensorSum(place, d_xs, d_xr, d_ys, d_yr, d_send, d_recv)
     base_out = remote(
@@ -344,6 +342,16 @@
         copy.wait()
     base_out.start()
     tell(place, reach.at[0], 2)
+    loads = []
+    for source, target in ((query_hbm, qs), (grad_hbm, dos)):
+        for h in range(heads):
+            for p in range(2):
+                loads.append(
+                    fetch(
+                        source.at[pl.ds(p * half, half), pl.ds(h * HEAD_SIZE, HEAD_SIZE)],
+                        target.at[p, pl.ds(h * half, half), :],
+                    )
+                )
 
     key_ids = lax.broadcasted_iota(jnp.int32, (half, tokens), 0)
     lanes = lax.broadcasted_iota(jnp.int32, (half, tokens), 1)
@@ -390,13 +398,14 @@
         ).astype(BF16),
     )
 
-    def unit(first, count, p, pair):
+    def products(first, count, p, pair):
         rows = slice(pair * tokens, (pair + 1) * tokens)
         keys = kv[0, first : first + count, :]
         values = kv[1, first : first + count, :]
-        queries = qs[p, rows, :]
-        grads = dos[p, rows, :]
-        scores = mul(keys, queries, NT) * (SCALE * LOG2E)
+        return mul(keys, qs[p, rows, :], NT), mul(values, dos[p, rows, :], NT)
+
+    def finish(first, count, p, pair, scores, prob_grad):
+        scores = scores * (SCALE * LOG2E)
         if count > half:
             scores = jnp.concatenate([scores[:half], scores[half:] + bias[...]], axis=0)
         else:
@@ -405,13 +414,23 @@
         weights = jnp.exp2(scores - highest)
         probs = weights * (1.0 / jnp.sum(weights, axis=0, keepdims=True))
         probs_low = probs.astype(BF16)
-        prob_grad = mul(values, grads, NT)
         row_dot = jnp.sum(probs * prob_grad, axis=0, keepdims=True)
         score_grad = (probs * (prob_grad - row_dot) * SCALE).astype(BF16)
-        outs[p, rows, :] = mul(values, probs_low, TN).T.astype(BF16)
+        return probs_low, score_grad
+
+    def spread(first, count, p, pair, probs_low, score_grad):
+        rows = slice(pair * tokens, (pair + 1) * tokens)
+        keys = kv[0, first : first + count, :]
+        values = kv[1, first : first + count, :]
+        result = mul(values, probs_low, TN).T.astype(BF16)
+        for e in range(2):
+            h = 2 * pair + e
+            outs[p * half : (p + 1) * half, h * HEAD_SIZE : (h + 1) * HEAD_SIZE] = result[
+                e * half : (e + 1) * half
+            ]
         query_grad = mul(keys, score_grad, TN).astype(BF16)
-        dkv[0, pad + first : pad + first + count, :] += mul(score_grad, queries)
-        dkv[1, pad + first : pad + first + count, :] += mul(probs_low, grads)
+        dkv[0, pad + first : pad + first + count, :] += mul(score_grad, qs[p, rows, :])
+        dkv[1, pad + first : pad + first + count, :] += mul(probs_low, dos[p, rows, :])
         one, two = 2 * pair, 2 * pair + 1
         ups = jnp.concatenate(
             [up_ref[:, h * HEAD_SIZE : (h + 1) * HEAD_SIZE] for h in (one, two)], axis=0
@@ -419,23 +438,30 @@
         rank_acc[p] += mul(ups, query_grad)
         up_acc[pair] += mul(wide_low[p], query_grad, NT)
 
-    unit(half, tokens, 1, 0)
-    unit(half, tokens, 1, 1)
+    def units(*which):
+        ready, done = [products(*which[0])], []
+        for k, one in enumerate(which):
+            if k + 1 < len(which):
+                ready.append(products(*which[k + 1]))
+            done.append(finish(*one, *ready[k]))
+            if k:
+                spread(*which[k - 1], *done[k - 1])
+        spread(*which[-1], *done[-1])
+
+    pl.semaphore_wait(reach.at[1], 2)
+    tell(place, reach.at[2], 8)
+    units((half, tokens, 1, 0), (half, tokens, 1, 1))
     base_out.wait()
     for i in range(2):
         low_out[i].wait()
         step = adapter_scale * mul(low_r[i], pair_ref[i], TN)
         kv[i, :half, :] = (base_r[i].astype(F32) + step[pad:]).astype(BF16)
-    unit(0, tokens, 0, 2)
-    unit(0, tokens, 0, 3)
+    units((0, tokens, 0, 2), (0, tokens, 0, 3))
     far_grads = [dkv[i, :tail, :].astype(BF16) for i in range(2)]
     for i in range(2):
         back_s[i] = mul(pair_ref[i], far_grads[i], NT).astype(BF16)
     back.start()
-    unit(half, half, 0, 0)
-    unit(half, half, 0, 1)
-    unit(tokens, half, 1, 2)
-    unit(tokens, half, 1, 3)
+    units((half, half, 0, 0), (half, half, 0, 1), (tokens, half, 1, 2), (tokens, half, 1, 3))
 
     first, second = rank_acc[0], rank_acc[1]
     ours = first[:depth] + pltpu.roll(first[depth:], half, 1)
@@ -461,51 +487,57 @@
     for c in range(3):
         rank_grads.middle(c)
     early.start()
-    pl.semaphore_wait(reach.at[1], 2)
-    tell(place, reach.at[2], 8)
     rank_grad = jnp.concatenate(
-        [(adapter_scale * rank_grads.end(c)).astype(BF16) for c in range(3)], axis=0
+        [(adapter_scale * rank_grads.end(c)).astype(BF16) for c in range(2)], axis=0
     )
     for j in range(8):
-        columns = slice(128 * j, 128 * j + 128)
-        down = mul(rank_grad, normed[:, columns])
-        g_mine[2 * j] = down[:24].astype(BF16)
-        g_mine[2 * j + 1] = down[24:].astype(BF16)
+        piece = mul(rank_grad, normed[:, 128 * j : 128 * j + 128]).astype(BF16)
+        g_mine[2 * j] = piece[:16]
+        g_mine[2 * j + 1] = piece[16:]
     late.start()
     pl.semaphore_wait(reach.at[2], 2)
     early.middle()
+    rank_grad = (adapter_scale * rank_grads.end(2)).astype(BF16)
+    for j in range(8):
+        piece = mul(rank_grad, normed[:, 128 * j : 128 * j + 128])
+        h_mine[2 * j] = piece[:8].astype(BF16)
+        h_mine[2 * j + 1] = piece[8:].astype(BF16)
+    last.start()
     late.middle()
+    last.middle()
     early.late()
+    late.late()
+    last.late()
     early.end()
     for c in range(16):
         value = e_full[c].astype(F32)
         up_out[8 * (c % 2) : 8 * (c % 2) + 8, 128 * (c // 2) : 128 * (c // 2) + 128] = value[:8]
         if c < 4:
             pair_out[8 * c : 8 * c + 8, :] = value[8:]
-    late.late()
     late.end()
     for c in range(16):
-        down_out[24 * (c % 2) : 24 * (c % 2) + 24, 128 * (c // 2) : 128 * (c // 2) + 128] = g_full[
-            c
-        ].astype(F32)
+        columns = slice(128 * (c // 2), 128 * (c // 2) + 128)
+        down_out[16 * (c % 2) : 16 * (c % 2) + 16, columns] = g_full[c].astype(F32)
+    last.end()
+    for c in range(16):
+        columns = slice(128 * (c // 2), 128 * (c // 2) + 128)
+        top = 32 + 8 * (c % 2)
+        down_out[top : top + 8, columns] = h_full[c].astype(F32)
     early.drain()
     late.drain()
+    last.drain()
 
 
 def store_kernel(outs, down, up, pair, attended_hbm, down_hbm, up_hbm, pair_hbm, sem):
-    half = attended_hbm.shape[0] // 2
-    heads = attended_hbm.shape[1] // HEAD_SIZE
-    copies = [
-        pltpu.make_async_copy(
-            outs.at[p, pl.ds(h * half, half), :],
-            attended_hbm.at[pl.ds(p * half, half), pl.ds(h * HEAD_SIZE, HEAD_SIZE)],
-            sem.at[2 * h + p],
+    rows = attended_hbm.shape[0] // STORES
+    copies = []
+    for k in range(STORES):
+        part = pl.ds(k * rows, rows)
+        copies.append(
+            pltpu.make_async_copy(outs.at[part], attended_hbm.at[part], sem.at[3 + k])
         )
-        for h in range(heads)
-        for p in range(2)
-    ]
     for k, (source, target) in enumerate(((down, down_hbm), (up, up_hbm), (pair, pair_hbm))):
-        copies.append(pltpu.make_async_copy(source, target, sem.at[2 * heads + k]))
+        copies.append(pltpu.make_async_copy(source, target, sem.at[k]))
     for copy in copies:
         copy.start()
     for copy in copies:
@@ -547,7 +579,7 @@
     results = pl.pallas_call(
         kernel,
         out_shape=(
-            pltpu.VMEM(stacked, BF16),
+            pltpu.VMEM((tokens, width), BF16),
             pltpu.VMEM((ranks, width), F32),
             pltpu.VMEM((depth, width), F32),
             pltpu.VMEM((2 * depth, HEAD_SIZE), F32),
@@ -580,7 +612,8 @@
         + tensor_sum_scratch(3, depth, tokens)
         + tensor_sum_scratch(3, depth, tokens)
         + token_sum_scratch(16)
-        + token_sum_scratch(24),
+        + token_sum_scratch(16)
+        + token_sum_scratch(8),
         compiler_params=pltpu.CompilerParams(
             collective_id=0, has_side_effects=True, vmem_limit_bytes=60 * 1024 * 1024
         ),
@@ -595,7 +628,7 @@
         ),
         in_specs=[vmem] * 4,
         out_specs=(hbm,) * 4,
-        scratch_shapes=[pltpu.SemaphoreType.DMA((2 * heads + 3,))],
+        scratch_shapes=[pltpu.SemaphoreType.DMA((3 + STORES,))],
         compiler_params=pltpu.CompilerParams(vmem_limit_bytes=1024 * 1024),
     )(*results)
     return (attended[None], down_grad.T, up_grad, pair_grad.reshape(2, depth, -1))

time: 71.1 us -> 72.1 us (1.014)
  Pallas kernels: 70.3 us -> 71.3 us
    pallas_call x1, Pallas kernels: 69.2 us -> 70.3 us  [on_device(): pl.pallas_call(kernel, out_shape=(pltpu.VMEM((tokens, width), BF16), pltp...]
where the time goes in v4:
time: 72.1 us; the launch traced here: 71.9 us
  Pallas kernels  71.3 us (99%)
    pallas_call x1, Pallas kernels, on_device(): pl.pallas_call(kernel, out_shape=(pltpu.VMEM((tokens, width), BF16), pltp...  70.3 us

profile of v4, /device:TPU:1, one launch (start us, length us, event | category | flops | bytes accessed | tf_op | source)
XLA Modules:
  0.0 71.9 jit_solution(6826088304256280837)
XLA Ops:
  0.6 70.3 %shard_map.111 = (bf16[384,1024]{1,0:T(8,128)(2,1)S(1)}, f32[48,1024]{1,0:T(8,128)S(1)}, f32[16,1024]{1,0:T(8,128)S(1)}, f32[32,128]{1,0:T(8,128)S(1)}) custom-call(bf16[384,1024]{1,0:T(8,128)(2,1)} %bitcast.9, bf16[384,1024]{1,0:T(8,128)(2,1)} %bitcast.10, bf16[384,128]{1,0:T(8,128)(2,1)} %bitcast.12, bf16[384,128]{1,0:T(8,128)(2,1)} %bitcast.13, ...), custom_call_target="tpu_custom_call" | custom-call | tf_op jit(solution)/shard_map/pallas_call | solution.py:579
  70.9 1.0 %shard_map.112 = (bf16[384,1024]{1,0:T(8,128)(2,1)}, f32[48,1024]{1,0:T(8,128)}, f32[16,1024]{1,0:T(8,128)}, f32[32,128]{1,0:T(8,128)}) custom-call(bf16[384,1024]{1,0:T(8,128)(2,1)S(1)} %get-tuple-element.12.outs, f32[48,1024]{1,0:T(8,128)S(1)} %get-tuple-element.13.down, f32[16,1024]{1,0:T(8,128)S(1)} %get-tuple-element.14.up, ...), custom_call_target="tpu_custom_call" | custom-call | tf_op jit(solution)/shard_map/pallas_call | solution.py:621

commit v5 on v4

--- a/solution.py
+++ b/solution.py
@@ -48,11 +48,11 @@
 
 
 def near_partners():
-    for i, step in enumerate(STEPS):
+    for step in STEPS:
         for a in (1, 0):
             for b in (1, 0):
                 if a or b or step:
-                    yield a, b, (-step if step == 2 and b else step), (a * 2 + b) * 4 + i
+                    yield a, b, step, (a * 2 + b) * 4 + STEPS.index(step)
 
 
 def remote(src, dst, send_sem, recv_sem, device):
@@ -277,12 +277,6 @@
     g_full,
     gsend,
     grecv,
-    h_mine,
-    h_got,
-    h_spread,
-    h_full,
-    hsend,
-    hrecv,
 ):
     place = Place()
     tokens, width = normed.shape
@@ -310,7 +304,6 @@
 
     early = TokenSum(place, e_mine, e_got, e_spread, e_full, esend, erecv)
     late = TokenSum(place, g_mine, g_got, g_spread, g_full, gsend, grecv)
-    last = TokenSum(place, h_mine, h_got, h_spread, h_full, hsend, hrecv)
     ranks = TensorSum(place, a_xs, a_xr, a_ys, a_yr, a_send, a_recv)
     rank_grads = TensorSum(place, d_xs, d_xr, d_ys, d_yr, d_send, d_recv)
     base_out = remote(
@@ -488,26 +481,19 @@
         rank_grads.middle(c)
     early.start()
     rank_grad = jnp.concatenate(
-        [(adapter_scale * rank_grads.end(c)).astype(BF16) for c in range(2)], axis=0
+        [(adapter_scale * rank_grads.end(c)).astype(BF16) for c in range(3)], axis=0
     )
     for j in range(8):
-        piece = mul(rank_grad, normed[:, 128 * j : 128 * j + 128]).astype(BF16)
-        g_mine[2 * j] = piece[:16]
-        g_mine[2 * j + 1] = piece[16:]
+        columns = slice(128 * j, 128 * j + 128)
+        down = mul(rank_grad, normed[:, columns])
+        g_mine[2 * j] = down[:24].astype(BF16)
+        g_mine[2 * j + 1] = down[24:].astype(BF16)
     late.start()
     pl.semaphore_wait(reach.at[2], 2)
     early.middle()
-    rank_grad = (adapter_scale * rank_grads.end(2)).astype(BF16)
-    for j in range(8):
-        piece = mul(rank_grad, normed[:, 128 * j : 128 * j + 128])
-        h_mine[2 * j] = piece[:8].astype(BF16)
-        h_mine[2 * j + 1] = piece[8:].astype(BF16)
-    last.start()
     late.middle()
-    last.middle()
     early.late()
     late.late()
-    last.late()
     early.end()
     for c in range(16):
         value = e_full[c].astype(F32)
@@ -516,16 +502,11 @@
             pair_out[8 * c : 8 * c + 8, :] = value[8:]
     late.end()
     for c in range(16):
-        columns = slice(128 * (c // 2), 128 * (c // 2) + 128)
-        down_out[16 * (c % 2) : 16 * (c % 2) + 16, columns] = g_full[c].astype(F32)
-    last.end()
-    for c in range(16):
-        columns = slice(128 * (c // 2), 128 * (c // 2) + 128)
-        top = 32 + 8 * (c % 2)
-        down_out[top : top + 8, columns] = h_full[c].astype(F32)
+        down_out[24 * (c % 2) : 24 * (c % 2) + 24, 128 * (c // 2) : 128 * (c // 2) + 128] = g_full[
+            c
+        ].astype(F32)
     early.drain()
     late.drain()
-    last.drain()
 
 
 def store_kernel(outs, down, up, pair, attended_hbm, down_hbm, up_hbm, pair_hbm, sem):
@@ -612,8 +593,7 @@
         + tensor_sum_scratch(3, depth, tokens)
         + tensor_sum_scratch(3, depth, tokens)
         + token_sum_scratch(16)
-        + token_sum_scratch(16)
-        + token_sum_scratch(8),
+        + token_sum_scratch(24),
         compiler_params=pltpu.CompilerParams(
             collective_id=0, has_side_effects=True, vmem_limit_bytes=60 * 1024 * 1024
         ),

time: 72.1 us -> 70.4 us (0.976)
  Pallas kernels: 71.3 us -> 69.6 us
    pallas_call x1, Pallas kernels: 70.3 us -> 68.5 us  [on_device(): pl.pallas_call(kernel, out_shape=(pltpu.VMEM((tokens, width), BF16), pltp...]
where the time goes in v5:
time: 70.4 us; the launch traced here: 70.2 us
  Pallas kernels  69.6 us (99%)
    pallas_call x1, Pallas kernels, on_device(): pl.pallas_call(kernel, out_shape=(pltpu.VMEM((tokens, width), BF16), pltp...  68.5 us

profile of v5, /device:TPU:1, one launch (start us, length us, event | category | flops | bytes accessed | tf_op | source)
XLA Modules:
  0.0 70.2 jit_solution(7267049005006780400)
XLA Ops:
  0.6 68.5 %shard_map.111 = (bf16[384,1024]{1,0:T(8,128)(2,1)S(1)}, f32[48,1024]{1,0:T(8,128)S(1)}, f32[16,1024]{1,0:T(8,128)S(1)}, f32[32,128]{1,0:T(8,128)S(1)}) custom-call(bf16[384,1024]{1,0:T(8,128)(2,1)} %bitcast.9, bf16[384,1024]{1,0:T(8,128)(2,1)} %bitcast.10, bf16[384,128]{1,0:T(8,128)(2,1)} %bitcast.12, bf16[384,128]{1,0:T(8,128)(2,1)} %bitcast.13, ...), custom_call_target="tpu_custom_call" | custom-call | tf_op jit(solution)/shard_map/pallas_call | solution.py:560
  69.2 1.0 %shard_map.112 = (bf16[384,1024]{1,0:T(8,128)(2,1)}, f32[48,1024]{1,0:T(8,128)}, f32[16,1024]{1,0:T(8,128)}, f32[32,128]{1,0:T(8,128)}) custom-call(bf16[384,1024]{1,0:T(8,128)(2,1)S(1)} %get-tuple-element.12.outs, f32[48,1024]{1,0:T(8,128)S(1)} %get-tuple-element.13.down, f32[16,1024]{1,0:T(8,128)S(1)} %get-tuple-element.14.up, ...), custom_call_target="tpu_custom_call" | custom-call | tf_op jit(solution)/shard_map/pallas_call | solution.py:601
